TPU v7x, 32 devices: a whole 2x2x4 slice. The times are simulated.
32 devices in a mesh: ctx: 16 (over z, y, x), tp: 2 (over core).
Axes of the slice: x: 2, y: 2, z: 4, core: 2. Of those that a mesh axis runs over, the one named last changes fastest.
Arguments:
- tokens: bfloat16 [4, 2048, 1280], P(None, 'ctx'), may hold values from -6 to 6
- cotangent: bfloat16 [4, 2048, 1280], P(None, 'ctx'), may hold values from -6 to 6
- doc_lengths: int32 [4, 8], replicated, may hold values from 1 to 1536, 2048 in all within a row
- w_query: bfloat16 [1280, 1280], P('ctx', 'tp'), may hold values from -0.15625 to 0.15625
- w_key: bfloat16 [1280, 1280], P('ctx', 'tp'), may hold values from -0.15625 to 0.15625
- w_value: bfloat16 [1280, 1280], P('ctx', 'tp'), may hold values from -0.15625 to 0.15625
- w_out: bfloat16 [1280, 1280], P('tp', 'ctx'), may hold values from -0.625 to 0.625
- w_up: bfloat16 [1280, 1280], P('ctx', 'tp'), may hold values from -0.15625 to 0.15625
- w_down: bfloat16 [1280, 1280], P('tp', 'ctx'), may hold values from -0.25 to 0.25
- gain_attn: bfloat16 [1280], P('ctx'), may hold values from 0.099609375 to 1.8984375
- gain_mlp: bfloat16 [1280], P('ctx'), may hold values from 0.099609375 to 1.8984375
- query_scale: float32 [80], replicated, may hold values from 0.06 to 0.3
Outputs:
- layer_out: bfloat16 [4, 2048, 1280], P(None, 'ctx')
- grad_tokens: float32 [4, 2048, 1280], P(None, 'ctx')
- grad_query: float32 [1280, 1280], P('ctx', 'tp')
- grad_key: float32 [1280, 1280], P('ctx', 'tp')
- grad_value: float32 [1280, 1280], P('ctx', 'tp')
- grad_out: float32 [1280, 1280], P('tp', 'ctx')
- grad_up: float32 [1280, 1280], P('ctx', 'tp')
- grad_down: float32 [1280, 1280], P('tp', 'ctx')
- grad_gain_attn: float32 [1280], P('ctx')
- grad_gain_mlp: float32 [1280], P('ctx')
- grad_scale: float32 [80], replicated
Inputs may be any that keep to these rules, and one draw needn't show every extreme that they name: `doc_lengths`: each row holds the lengths of the 8 documents of one stream in order; they sum to 2048, and the longest is exactly 1536.
All inputs are finite; a program needn't handle non-finite values.
Results may differ from a plain program's by a relative error of at most 0.024.
Values may be sent and summed in bfloat16 or wider, within the bound.
No kernel may reach another device: no remote copies, remote signals or barrier semaphores. Data moves between devices by JAX's collectives and lax.ppermute only.
A program may use at most 192 MiB of HBM per device.

v0:
```python
import jax
import jax.numpy as jnp
from jax import lax
from jax.sharding import PartitionSpec as P

EPSILON = 1e-06
MASKED = -1e30


def inverse_rms(values):
    return lax.rsqrt(jnp.mean(values * values, axis=-1, keepdims=True) + EPSILON)


def segment_of(starts, positions):
    return jnp.sum((starts[None, :] <= positions[:, None]).astype(jnp.int32), axis=1)


def contract_rows(left, right):
    return lax.dot_general(
        left, right, (((0,), (0,)), ((), ())), preferred_element_type=jnp.float32
    )


def contract_cols(left, right):
    return lax.dot_general(
        left, right, (((1,), (1,)), ((), ())), preferred_element_type=jnp.float32
    )


def per_device(
    tokens,
    cotangent,
    doc_lengths,
    w_query,
    w_key,
    w_value,
    w_out,
    w_up,
    w_down,
    gain_attn,
    gain_mlp,
    query_scale,
):
    micro_count, tok_rows, model_width = tokens.shape
    head_size = query_scale.shape[0]
    local_cols = w_query.shape[1]
    head_count = local_cols // head_size
    stream = tok_rows * lax.axis_size("ctx")
    key_block = min(512, stream)
    block_count = stream // key_block
    positions = lax.axis_index("ctx") * tok_rows + jnp.arange(tok_rows, dtype=jnp.int32)
    local_sums = None
    scale_sum = jnp.zeros((head_size,), jnp.float32)
    outputs = []
    input_grads = []
    for micro_step in range(micro_count):
        gathered = (
            lax.all_gather(w_query, "ctx", axis=0, tiled=True),
            lax.all_gather(w_key, "ctx", axis=0, tiled=True),
            lax.all_gather(w_value, "ctx", axis=0, tiled=True),
            lax.all_gather(w_up, "ctx", axis=0, tiled=True),
            lax.all_gather(gain_attn, "ctx", axis=0, tiled=True),
            lax.all_gather(gain_mlp, "ctx", axis=0, tiled=True),
            lax.all_gather(w_out, "ctx", axis=1, tiled=True),
            lax.all_gather(w_down, "ctx", axis=1, tiled=True),
        )
        w_qkv = jnp.concatenate([gathered[0], gathered[1], gathered[2]], axis=1)
        up_full = gathered[3]
        gain_one = gathered[4].astype(jnp.float32)
        gain_two = gathered[5].astype(jnp.float32)
        out_full = gathered[6]
        down_full = gathered[7]
        lengths = doc_lengths[micro_step]
        starts = jnp.cumsum(lengths) - lengths
        query_seg = segment_of(starts, positions)
        stream_in = tokens[micro_step].astype(jnp.float32)
        scale_one = inverse_rms(stream_in)
        normed_one = (stream_in * scale_one * gain_one).astype(jnp.bfloat16)
        projected = jnp.dot(normed_one, w_qkv, preferred_element_type=jnp.float32)
        query_raw = projected[:, :local_cols].reshape(tok_rows, head_count, head_size)
        query_heads = (query_raw * query_scale).astype(jnp.bfloat16)
        key_local = projected[:, local_cols : 2 * local_cols].astype(jnp.bfloat16)
        value_local = projected[:, 2 * local_cols :].astype(jnp.bfloat16)
        row_top = jnp.full((head_count, tok_rows), MASKED, jnp.float32)
        key_piece = lax.all_gather(key_local, "ctx", axis=0, tiled=True)
        value_piece = lax.all_gather(value_local, "ctx", axis=0, tiled=True)
        length = key_piece.shape[0]
        key_pos = jnp.arange(length, dtype=jnp.int32)
        allowed = (key_pos[None, :] <= positions[:, None]) & (
            segment_of(starts, key_pos)[None, :] == query_seg[:, None]
        )
        scores = jnp.einsum(
            "qhd,khd->hqk",
            query_heads,
            key_piece.reshape(length, head_count, head_size),
            preferred_element_type=jnp.float32,
        )
        scores = jnp.where(allowed[None], scores, MASKED)
        new_top = jnp.maximum(row_top, jnp.max(scores, axis=-1))
        probs = jnp.where(allowed[None], jnp.exp(scores - new_top[:, :, None]), 0.0)
        row_sum = jnp.sum(probs, axis=-1)
        update = jnp.einsum(
            "hqk,khd->qhd",
            probs.astype(jnp.bfloat16),
            value_piece.reshape(length, head_count, head_size),
            preferred_element_type=jnp.float32,
        )
        weighted = update
        row_top, row_sum, weighted = (new_top, row_sum, weighted)
        attn_heads = weighted / jnp.transpose(row_sum)[:, :, None]
        log_total = row_top + jnp.log(row_sum)
        attn_low = attn_heads.reshape(tok_rows, local_cols).astype(jnp.bfloat16)
        attn_out = lax.psum(
            jnp.dot(attn_low, out_full, preferred_element_type=jnp.float32).astype(jnp.bfloat16),
            "tp",
        ).astype(jnp.float32)
        hidden = stream_in + attn_out
        scale_two = inverse_rms(hidden)
        normed_two = (hidden * scale_two * gain_two).astype(jnp.bfloat16)
        up_raw = jnp.dot(normed_two, up_full, preferred_element_type=jnp.float32)
        activated = jax.nn.silu(up_raw).astype(jnp.bfloat16)
        mlp_out = lax.psum(
            jnp.dot(activated, down_full, preferred_element_type=jnp.float32).astype(jnp.bfloat16),
            "tp",
        ).astype(jnp.float32)
        outputs.append((hidden + mlp_out).astype(jnp.bfloat16))
        grad_out = cotangent[micro_step]
        grad_down = contract_rows(activated, grad_out)
        grad_act = contract_cols(grad_out, down_full)
        sigma = jax.nn.sigmoid(up_raw)
        grad_up_raw = (grad_act * sigma * (1.0 + up_raw * (1.0 - sigma))).astype(jnp.bfloat16)
        grad_up = contract_rows(normed_two, grad_up_raw)
        grad_normed_two = lax.psum(
            contract_cols(grad_up_raw, up_full).astype(jnp.bfloat16), "tp"
        ).astype(jnp.float32)
        grad_gain_two = jnp.sum(grad_normed_two * hidden * scale_two, axis=0)
        weighted_two = grad_normed_two * gain_two
        grad_hidden = (
            grad_out.astype(jnp.float32)
            + scale_two * weighted_two
            - hidden * scale_two**3 * jnp.mean(weighted_two * hidden, axis=-1, keepdims=True)
        )
        hidden_low = grad_hidden.astype(jnp.bfloat16)
        grad_out_proj = contract_rows(attn_low, hidden_low)
        grad_attn = (
            contract_cols(hidden_low, out_full)
            .astype(jnp.bfloat16)
            .reshape(tok_rows, head_count, head_size)
        )
        delta = jnp.einsum("qhd,qhd->hq", grad_attn.astype(jnp.float32), attn_heads)
        key_all, value_all = (
            lax.all_gather(key_local, "ctx", axis=0, tiled=True),
            lax.all_gather(value_local, "ctx", axis=0, tiled=True),
        )

        def block_terms(key_piece, value_piece, offset):
            key_heads = key_piece.reshape(key_block, head_count, head_size)
            value_heads = value_piece.reshape(key_block, head_count, head_size)
            key_pos = offset + jnp.arange(key_block, dtype=jnp.int32)
            allowed = (key_pos[None, :] <= positions[:, None]) & (
                segment_of(starts, key_pos)[None, :] == query_seg[:, None]
            )
            scores = jnp.einsum(
                "qhd,khd->hqk", query_heads, key_heads, preferred_element_type=jnp.float32
            )
            probs = jnp.where(allowed[None], jnp.exp(scores - log_total[:, :, None]), 0.0)
            grad_probs = jnp.einsum(
                "qhd,khd->hqk", grad_attn, value_heads, preferred_element_type=jnp.float32
            )
            grad_scores = (probs * (grad_probs - delta[:, :, None])).astype(jnp.bfloat16)
            return (key_heads, probs, grad_scores)

        key_blocks = (
            key_all.reshape(block_count, key_block, local_cols),
            value_all.reshape(block_count, key_block, local_cols),
            jnp.arange(block_count, dtype=jnp.int32) * key_block,
        )
        zero_query = jnp.zeros((tok_rows, head_count, head_size), jnp.float32)

        def grad_block(grad_query, packed):
            key_heads, probs, grad_scores = block_terms(packed[0], packed[1], packed[2])
            grad_value = jnp.einsum(
                "hqk,qhd->khd",
                probs.astype(jnp.bfloat16),
                grad_attn,
                preferred_element_type=jnp.float32,
            )
            grad_query = grad_query + jnp.einsum(
                "hqk,khd->qhd", grad_scores, key_heads, preferred_element_type=jnp.float32
            )
            grad_key = jnp.einsum(
                "hqk,qhd->khd", grad_scores, query_heads, preferred_element_type=jnp.float32
            )
            return (
                grad_query,
                (
                    grad_key.reshape(key_block, local_cols),
                    grad_value.reshape(key_block, local_cols),
                ),
            )

        grad_query, (key_terms, value_terms) = lax.scan(grad_block, zero_query, key_blocks)
        key_grad, value_grad = (
            lax.psum_scatter(
                key_terms.reshape(stream, local_cols).astype(jnp.bfloat16),
                "ctx",
                scatter_dimension=0,
                tiled=True,
            ).astype(jnp.float32),
            lax.psum_scatter(
                value_terms.reshape(stream, local_cols).astype(jnp.bfloat16),
                "ctx",
                scatter_dimension=0,
                tiled=True,
            ).astype(jnp.float32),
        )
        grad_query_raw = (
            (grad_query * query_scale).astype(jnp.bfloat16).reshape(tok_rows, local_cols)
        )
        scale_part = jnp.sum(grad_query * query_raw, axis=(0, 1))
        grad_cols = jnp.concatenate(
            [grad_query_raw, key_grad.astype(jnp.bfloat16), value_grad.astype(jnp.bfloat16)], axis=1
        )
        grad_qkv = contract_rows(normed_one, grad_cols)
        grad_normed_one, scale_total = (
            lax.psum(contract_cols(grad_cols, w_qkv).astype(jnp.bfloat16), "tp").astype(
                jnp.float32
            ),
            lax.psum(scale_part.astype(jnp.bfloat16), "tp").astype(jnp.float32),
        )
        scale_sum = scale_sum + scale_total
        grad_gain_one = jnp.sum(grad_normed_one * stream_in * scale_one, axis=0)
        weighted_one = grad_normed_one * gain_one
        input_grads.append(
            grad_hidden
            + scale_one * weighted_one
            - stream_in * scale_one**3 * jnp.mean(weighted_one * stream_in, axis=-1, keepdims=True)
        )
        grads = (
            grad_qkv[:, :local_cols],
            grad_qkv[:, local_cols : 2 * local_cols],
            grad_qkv[:, 2 * local_cols :],
            grad_up,
            grad_gain_one,
            grad_gain_two,
            grad_out_proj,
            grad_down,
        )
        shares = (
            lax.psum_scatter(
                grads[0].astype(jnp.bfloat16), "ctx", scatter_dimension=0, tiled=True
            ).astype(jnp.float32),
            lax.psum_scatter(
                grads[1].astype(jnp.bfloat16), "ctx", scatter_dimension=0, tiled=True
            ).astype(jnp.float32),
            lax.psum_scatter(
                grads[2].astype(jnp.bfloat16), "ctx", scatter_dimension=0, tiled=True
            ).astype(jnp.float32),
            lax.psum_scatter(
                grads[3].astype(jnp.bfloat16), "ctx", scatter_dimension=0, tiled=True
            ).astype(jnp.float32),
            lax.psum_scatter(
                grads[4].astype(jnp.bfloat16), "ctx", scatter_dimension=0, tiled=True
            ).astype(jnp.float32),
            lax.psum_scatter(
                grads[5].astype(jnp.bfloat16), "ctx", scatter_dimension=0, tiled=True
            ).astype(jnp.float32),
            lax.psum_scatter(
                grads[6].astype(jnp.bfloat16), "ctx", scatter_dimension=1, tiled=True
            ).astype(jnp.float32),
            lax.psum_scatter(
                grads[7].astype(jnp.bfloat16), "ctx", scatter_dimension=1, tiled=True
            ).astype(jnp.float32),
        )
        local_sums = (
            shares
            if local_sums is None
            else tuple((total + extra for total, extra in zip(local_sums, shares)))
        )
    scale_grad = lax.psum(scale_sum, "ctx")
    return (
        jnp.stack(outputs),
        jnp.stack(input_grads),
        local_sums[0],
        local_sums[1],
        local_sums[2],
        local_sums[6],
        local_sums[3],
        local_sums[7],
        local_sums[4],
        local_sums[5],
        scale_grad,
    )


def solution(mesh):
    in_specs = (
        P(None, "ctx", None),
        P(None, "ctx", None),
        P(),
        P("ctx", "tp"),
        P("ctx", "tp"),
        P("ctx", "tp"),
        P("tp", "ctx"),
        P("ctx", "tp"),
        P("tp", "ctx"),
        P("ctx"),
        P("ctx"),
        P(),
    )
    out_specs = (
        P(None, "ctx", None),
        P(None, "ctx", None),
        P("ctx", "tp"),
        P("ctx", "tp"),
        P("ctx", "tp"),
        P("tp", "ctx"),
        P("ctx", "tp"),
        P("tp", "ctx"),
        P("ctx"),
        P("ctx"),
        P(),
    )
    return jax.shard_map(
        per_device, mesh=mesh, in_specs=in_specs, out_specs=out_specs, check_vma=False
    )
```

profile of v0, /device:TPU:0, one launch (start us, length us, event | category | flops | bytes accessed | tf_op | source)
XLA Modules:
  0.0 3650.7 jit_solution(5075666711736154191)
XLA Ops:
  13.1 44.2 %all-reduce.11 = (bf16[1280]{0:T(1024)(128)(2,1)S(1)}, bf16[1280]{0:T(1024)(128)(2,1)S(1)}) all-reduce(bf16[1280]{0:T(1024)(128)(2,1)S(1)} %dynamic-update-slice, bf16[1280]{0:T(1024)(128)(2,1)S(1)} %dynamic-update-slice.1), channel_id=1, replica_groups=mesh['ctx'=16,'tp'=2] {'ctx'}, use_global_device_ids=true, to_apply=%add | all-reduce | flops 2560 | bytes 10240
  59.0 12.7 all-gather.15.cloned.1.call-done
  74.6 56.9 %all-gather.17.cloned.1.call-done = bf16[1280,640]{1,0:T(8,128)(2,1)} async-done(((bf16[80,640]{1,0:T(8,128)(2,1)}), bf16[1280,640]{1,0:T(8,128)(2,1)}) %all-gather.17.cloned.1.call-update) | async-done | bytes 1638416 | tf_op jit(solution)/shard_map/all_gather | solution.py:59
  134.3 56.9 %all-gather.19.cloned.1.call-done = bf16[1280,640]{1,0:T(8,128)(2,1)} async-done(((bf16[80,640]{1,0:T(8,128)(2,1)}), bf16[1280,640]{1,0:T(8,128)(2,1)}) %all-gather.19.cloned.1.call-update) | async-done | bytes 1638416 | tf_op jit(solution)/shard_map/all_gather | solution.py:60
  202.6 58.6 %all-gather.37.cloned.1.call-done = bf16[2048,640]{1,0:T(8,128)(2,1)} async-done(((bf16[128,640]{1,0:T(8,128)(2,1)}), bf16[2048,640]{1,0:T(8,128)(2,1)}) %all-gather.37.cloned.1.call-update) | async-done | bytes 2621456 | tf_op jit(solution)/shard_map/all_gather | solution.py:85
  265.5 61.7 %all-gather.35.cloned.1.call-done = bf16[2048,640]{1,0:T(8,128)(2,1)} async-done(((bf16[128,640]{1,0:T(8,128)(2,1)}), bf16[2048,640]{1,0:T(8,128)(2,1)}) %all-gather.35.cloned.1.call-update) | async-done | bytes 2621456 | tf_op jit(solution)/shard_map/all_gather | solution.py:86
  340.3 46.6 %all-gather.25.cloned.1.call-done = bf16[640,1280]{0,1:T(8,128)(2,1)} async-done(((bf16[640,80]{0,1:T(8,128)(2,1)}), bf16[640,1280]{0,1:T(8,128)(2,1)}) %all-gather.25.cloned.1.call-update) | async-done | bytes 1638416 | tf_op jit(solution)/shard_map/all_gather | solution.py:64
  391.2 15.8 all-reduce.21.cloned.1.call-done
  413.0 9.6 all-gather.23.cloned.1.call-start
  439.0 30.4 all-gather.27.cloned.1.call-done
  472.1 57.4 %all-gather.29.cloned.1.call-done = bf16[640,1280]{0,1:T(8,128)(2,1)} async-done(((bf16[640,80]{0,1:T(8,128)(2,1)}), bf16[640,1280]{0,1:T(8,128)(2,1)}) %all-gather.29.cloned.1.call-update) | async-done | bytes 1638416 | tf_op jit(solution)/shard_map/all_gather | solution.py:65
  533.4 62.4 %all-gather.41.cloned.1.call-done = bf16[2048,640]{1,0:T(8,128)(2,1)} async-done(((bf16[128,640]{1,0:T(8,128)(2,1)}), bf16[2048,640]{1,0:T(8,128)(2,1)}) %all-gather.41.cloned.1.call-update) | async-done | bytes 2621456 | tf_op jit(solution)/shard_map/all_gather | solution.py:85
  600.2 6.5 select_reduce_fusion
  606.7 55.7 %all-gather.23.cloned.1.call-done = bf16[2048,640]{1,0:T(8,128)(2,1)} async-done(((bf16[128,640]{1,0:T(8,128)(2,1)}), bf16[2048,640]{1,0:T(8,128)(2,1)}) %all-gather.23.cloned.1.call-update) | async-done | bytes 2621456 | tf_op jit(solution)/shard_map/all_gather | solution.py:85
  666.8 6.5 select_reduce_fusion.3
  673.3 55.6 %all-gather.39.cloned.1.call-done = bf16[2048,640]{1,0:T(8,128)(2,1)} async-done(((bf16[128,640]{1,0:T(8,128)(2,1)}), bf16[2048,640]{1,0:T(8,128)(2,1)}) %all-gather.39.cloned.1.call-update) | async-done | bytes 2621456 | tf_op jit(solution)/shard_map/all_gather | solution.py:86
  733.3 62.2 %all-gather.21.cloned.1.call-done = bf16[2048,640]{1,0:T(8,128)(2,1)} async-done(((bf16[128,640]{1,0:T(8,128)(2,1)}), bf16[2048,640]{1,0:T(8,128)(2,1)}) %all-gather.21.cloned.1.call-update) | async-done | bytes 2621456 | tf_op jit(solution)/shard_map/all_gather | solution.py:86
  795.5 4.5 copy.171
  800.0 62.0 %all-gather.33.cloned.1.call-done = bf16[2048,640]{1,0:T(8,128)(2,1)} async-done(((bf16[128,640]{1,0:T(8,128)(2,1)}), bf16[2048,640]{1,0:T(8,128)(2,1)}) %all-gather.33.cloned.1.call-update) | async-done | bytes 2621456 | tf_op jit(solution)/shard_map/all_gather | solution.py:85
  869.8 7.6 fusion.50
  877.4 4.7 fusion.44
  891.0 37.4 %all-gather.31.cloned.1.call-done = bf16[2048,640]{1,0:T(8,128)(2,1)} async-done(((bf16[128,640]{1,0:T(8,128)(2,1)}), bf16[2048,640]{1,0:T(8,128)(2,1)}) %all-gather.31.cloned.1.call-update) | async-done | bytes 2621456 | tf_op jit(solution)/shard_map/all_gather | solution.py:86
  932.8 7.0 fusion.270
  943.9 19.2 all-reduce.27.cloned.1.call-done
  975.7 19.6 all-reduce.25.cloned.1.call-done
  1006.0 70.7 %while.63 = (s32[]{:T(128)}, f32[128,8,80]{0,2,1:T(8,128)}, bf16[4,512,640]{2,1,0:T(8,128)(2,1)}, bf16[4,512,640]{2,1,0:T(8,128)(2,1)}, bf16[4,512,640]{2,1,0:T(...) while((s32[]{:T(128)}, f32[128,8,80]{0,2,1:T(8,128)}, ...), condition=%wide.region_67.68_spmd.clone, body=%wide.region_65.67_spmd.clone.sunk | while | flops 423997568 | bytes 31285108 | solution.py:202
  1087.4 71.6 %while.60 = (s32[]{:T(128)}, f32[128,8,80]{0,2,1:T(8,128)}, bf16[4,512,640]{2,1,0:T(8,128)(2,1)}, bf16[4,512,640]{2,1,0:T(8,128)(2,1)}, bf16[4,512,640]{2,1,0:T(...) while((s32[]{:T(128)}, f32[128,8,80]{0,2,1:T(8,128)}, ...), condition=%wide.region_40.41_spmd.clone, body=%wide.region_38.40_spmd.clone.sunk | while | flops 423997568 | bytes 30629728 | solution.py:202
  1166.3 71.5 %while.61 = (s32[]{:T(128)}, f32[128,8,80]{0,2,1:T(8,128)}, bf16[4,512,640]{2,1,0:T(8,128)(2,1)}, bf16[4,512,640]{2,1,0:T(8,128)(2,1)}, bf16[4,512,640]{2,1,0:T(...) while((s32[]{:T(128)}, f32[128,8,80]{0,2,1:T(8,128)}, ...), condition=%wide.region_49.50_spmd.clone, body=%wide.region_47.49_spmd.clone.sunk | while | flops 423997568 | bytes 30629728 | solution.py:202
  1245.1 70.9 %while.62 = (s32[]{:T(128)}, f32[128,8,80]{0,2,1:T(8,128)}, bf16[4,512,640]{2,1,0:T(8,128)(2,1)}, bf16[4,512,640]{2,1,0:T(8,128)(2,1)}, bf16[4,512,640]{2,1,0:T(...) while((s32[]{:T(128)}, f32[128,8,80]{0,2,1:T(8,128)}, ...), condition=%wide.region_58.59_spmd.clone, body=%wide.region_56.58_spmd.clone.sunk | while | flops 423997568 | bytes 30629728 | solution.py:202
  1361.8 4.8 convolution_convert_fusion.16
  1366.6 39.7 %reduce-scatter.33.cloned.1.call-done = bf16[128,640]{1,0:T(8,128)(2,1)} async-done(((bf16[2048,640]{1,0:T(8,128)(2,1)}), bf16[128,640]{1,0:T(8,128)(2,1)}) %reduce-scatter.33.cloned.1.call-update) | async-done | bytes 163856 | tf_op jit(solution)/shard_map/reduce_scatter | solution.py:204
  1406.3 4.8 convolution_convert_fusion.22
  1411.1 76.5 %reduce-scatter.39.cloned.1.call-done = bf16[128,640]{1,0:T(8,128)(2,1)} async-done(((bf16[2048,640]{1,0:T(8,128)(2,1)}), bf16[128,640]{1,0:T(8,128)(2,1)}) %reduce-scatter.39.cloned.1.call-update) | async-done | bytes 163856 | tf_op jit(solution)/shard_map/reduce_scatter | solution.py:210
  1487.6 82.2 %reduce-scatter.37.cloned.1.call-done = bf16[128,640]{1,0:T(8,128)(2,1)} async-done(((bf16[2048,640]{1,0:T(8,128)(2,1)}), bf16[128,640]{1,0:T(8,128)(2,1)}) %reduce-scatter.37.cloned.1.call-update) | async-done | bytes 163856 | tf_op jit(solution)/shard_map/reduce_scatter | solution.py:204
  1569.9 4.8 convolution_convert_fusion.20
  1574.6 76.9 %reduce-scatter.43.cloned.1.call-done = bf16[128,640]{1,0:T(8,128)(2,1)} async-done(((bf16[2048,640]{1,0:T(8,128)(2,1)}), bf16[128,640]{1,0:T(8,128)(2,1)}) %reduce-scatter.43.cloned.1.call-update) | async-done | bytes 163856 | tf_op jit(solution)/shard_map/reduce_scatter | solution.py:210
  1651.5 81.9 %reduce-scatter.41.cloned.1.call-done = bf16[128,640]{1,0:T(8,128)(2,1)} async-done(((bf16[2048,640]{1,0:T(8,128)(2,1)}), bf16[128,640]{1,0:T(8,128)(2,1)}) %reduce-scatter.41.cloned.1.call-update) | async-done | bytes 163856 | tf_op jit(solution)/shard_map/reduce_scatter | solution.py:204
  1733.5 4.8 convolution_convert_fusion.18
  1762.8 38.6 %psum.167 = f32[80]{0:T(128)} all-reduce(f32[80]{0:T(128)S(1)} %convert_add_fusion.10), channel_id=1, replica_groups=mesh['ctx'=16,'tp'=2] {'ctx'}, use_global_device_ids=true, to_apply=%region_120.121 | all-reduce | flops 80 | bytes 640 | tf_op jit(solution)/shard_map/psum | solution.py:280
  1801.4 10.8 reduce-scatter.85.cloned.1.call-done
  1812.3 78.3 %reduce-scatter.87.cloned.1.call-done = bf16[80,640]{1,0:T(8,128)(2,1)} async-done(((bf16[1280,640]{1,0:T(8,128)(2,1)}), bf16[80,640]{1,0:T(8,128)(2,1)}) %reduce-scatter.87.cloned.1.call-update) | async-done | bytes 102416 | tf_op jit(solution)/shard_map/reduce_scatter | solution.py:259
  1890.6 78.3 %reduce-scatter.83.cloned.1.call-done = bf16[80,640]{1,0:T(8,128)(2,1)} async-done(((bf16[1280,640]{1,0:T(8,128)(2,1)}), bf16[80,640]{1,0:T(8,128)(2,1)}) %reduce-scatter.83.cloned.1.call-update) | async-done | bytes 102416 | tf_op jit(solution)/shard_map/reduce_scatter | solution.py:259
  1968.9 78.5 %reduce-scatter.81.cloned.1.call-done = bf16[80,640]{1,0:T(8,128)(2,1)} async-done(((bf16[1280,640]{1,0:T(8,128)(2,1)}), bf16[80,640]{1,0:T(8,128)(2,1)}) %reduce-scatter.81.cloned.1.call-update) | async-done | bytes 102416 | tf_op jit(solution)/shard_map/reduce_scatter | solution.py:259
  2049.1 76.8 %reduce-scatter.93.cloned.1.call-done = bf16[640,80]{0,1:T(8,128)(2,1)} async-done(((bf16[640,1280]{0,1:T(8,128)(2,1)}), bf16[640,80]{0,1:T(8,128)(2,1)}) %reduce-scatter.93.cloned.1.call-update) | async-done | bytes 102416 | tf_op jit(solution)/shard_map/reduce_scatter | solution.py:271
  2125.9 78.3 %reduce-scatter.95.cloned.1.call-done = bf16[640,80]{0,1:T(8,128)(2,1)} async-done(((bf16[640,1280]{0,1:T(8,128)(2,1)}), bf16[640,80]{0,1:T(8,128)(2,1)}) %reduce-scatter.95.cloned.1.call-update) | async-done | bytes 102416 | tf_op jit(solution)/shard_map/reduce_scatter | solution.py:271
  2204.2 78.5 %reduce-scatter.91.cloned.1.call-done = bf16[640,80]{0,1:T(8,128)(2,1)} async-done(((bf16[640,1280]{0,1:T(8,128)(2,1)}), bf16[640,80]{0,1:T(8,128)(2,1)}) %reduce-scatter.91.cloned.1.call-update) | async-done | bytes 102416 | tf_op jit(solution)/shard_map/reduce_scatter | solution.py:271
  2282.7 78.2 %reduce-scatter.89.cloned.1.call-done = bf16[640,80]{0,1:T(8,128)(2,1)} async-done(((bf16[640,1280]{0,1:T(8,128)(2,1)}), bf16[640,80]{0,1:T(8,128)(2,1)}) %reduce-scatter.89.cloned.1.call-update) | async-done | bytes 102416 | tf_op jit(solution)/shard_map/reduce_scatter | solution.py:271
  2362.7 76.4 %reduce-scatter.79.cloned.1.call-done = bf16[640,80]{0,1:T(8,128)(2,1)} async-done(((bf16[640,1280]{0,1:T(8,128)(2,1)}), bf16[640,80]{0,1:T(8,128)(2,1)}) %reduce-scatter.79.cloned.1.call-update) | async-done | bytes 102416 | tf_op jit(solution)/shard_map/reduce_scatter | solution.py:268
  2439.1 78.5 %reduce-scatter.77.cloned.1.call-done = bf16[640,80]{0,1:T(8,128)(2,1)} async-done(((bf16[640,1280]{0,1:T(8,128)(2,1)}), bf16[640,80]{0,1:T(8,128)(2,1)}) %reduce-scatter.77.cloned.1.call-update) | async-done | bytes 102416 | tf_op jit(solution)/shard_map/reduce_scatter | solution.py:268
  2517.6 78.4 %reduce-scatter.75.cloned.1.call-done = bf16[640,80]{0,1:T(8,128)(2,1)} async-done(((bf16[640,1280]{0,1:T(8,128)(2,1)}), bf16[640,80]{0,1:T(8,128)(2,1)}) %reduce-scatter.75.cloned.1.call-update) | async-done | bytes 102416 | tf_op jit(solution)/shard_map/reduce_scatter | solution.py:268
  2596.0 78.4 %reduce-scatter.73.cloned.1.call-done = bf16[640,80]{0,1:T(8,128)(2,1)} async-done(((bf16[640,1280]{0,1:T(8,128)(2,1)}), bf16[640,80]{0,1:T(8,128)(2,1)}) %reduce-scatter.73.cloned.1.call-update) | async-done | bytes 102416 | tf_op jit(solution)/shard_map/reduce_scatter | solution.py:268
  2676.2 20.9 all-reduce.23.cloned.1.call-done
  2699.2 77.6 %all-reduce.10 = (bf16[1280]{0:T(1024)(128)(2,1)S(1)}, bf16[1280]{0:T(1024)(128)(2,1)S(1)}, bf16[1280]{0:T(1024)(128)(2,1)S(1)}, bf16[1280]{0:T(1024)(128)(2,1)S...) all-reduce(bf16[1280]{0:T(1024)(128)(2,1)S(1)} %get-tuple-element.7, ...), channel_id=37, replica_groups=mesh['ctx'=16,'tp'=2] {'ctx'}, use_global_device_ids=true, to_apply=%region_103.104.clone | all-reduce | flops 10240 | bytes 40960
  2784.7 73.9 %reduce-scatter.53.cloned.1.call-done = bf16[80,640]{1,0:T(8,128)(2,1)} async-done(((bf16[1280,640]{1,0:T(8,128)(2,1)}), bf16[80,640]{1,0:T(8,128)(2,1)}) %reduce-scatter.53.cloned.1.call-update) | async-done | bytes 102416 | tf_op jit(solution)/shard_map/reduce_scatter | solution.py:250
  2858.6 78.2 %reduce-scatter.51.cloned.1.call-done = bf16[80,640]{1,0:T(8,128)(2,1)} async-done(((bf16[1280,640]{1,0:T(8,128)(2,1)}), bf16[80,640]{1,0:T(8,128)(2,1)}) %reduce-scatter.51.cloned.1.call-update) | async-done | bytes 102416 | tf_op jit(solution)/shard_map/reduce_scatter | solution.py:250
  2936.8 78.5 %reduce-scatter.49.cloned.1.call-done = bf16[80,640]{1,0:T(8,128)(2,1)} async-done(((bf16[1280,640]{1,0:T(8,128)(2,1)}), bf16[80,640]{1,0:T(8,128)(2,1)}) %reduce-scatter.49.cloned.1.call-update) | async-done | bytes 102416 | tf_op jit(solution)/shard_map/reduce_scatter | solution.py:250
  3017.1 76.8 %reduce-scatter.63.cloned.1.call-done = bf16[80,640]{1,0:T(8,128)(2,1)} async-done(((bf16[1280,640]{1,0:T(8,128)(2,1)}), bf16[80,640]{1,0:T(8,128)(2,1)}) %reduce-scatter.63.cloned.1.call-update) | async-done | bytes 102416 | tf_op jit(solution)/shard_map/reduce_scatter | solution.py:253
  3093.8 78.4 %reduce-scatter.61.cloned.1.call-done = bf16[80,640]{1,0:T(8,128)(2,1)} async-done(((bf16[1280,640]{1,0:T(8,128)(2,1)}), bf16[80,640]{1,0:T(8,128)(2,1)}) %reduce-scatter.61.cloned.1.call-update) | async-done | bytes 102416 | tf_op jit(solution)/shard_map/reduce_scatter | solution.py:253
  3172.2 78.3 %reduce-scatter.59.cloned.1.call-done = bf16[80,640]{1,0:T(8,128)(2,1)} async-done(((bf16[1280,640]{1,0:T(8,128)(2,1)}), bf16[80,640]{1,0:T(8,128)(2,1)}) %reduce-scatter.59.cloned.1.call-update) | async-done | bytes 102416 | tf_op jit(solution)/shard_map/reduce_scatter | solution.py:253
  3250.6 78.3 %reduce-scatter.57.cloned.1.call-done = bf16[80,640]{1,0:T(8,128)(2,1)} async-done(((bf16[1280,640]{1,0:T(8,128)(2,1)}), bf16[80,640]{1,0:T(8,128)(2,1)}) %reduce-scatter.57.cloned.1.call-update) | async-done | bytes 102416 | tf_op jit(solution)/shard_map/reduce_scatter | solution.py:253
  3330.7 76.2 %reduce-scatter.71.cloned.1.call-done = bf16[80,640]{1,0:T(8,128)(2,1)} async-done(((bf16[1280,640]{1,0:T(8,128)(2,1)}), bf16[80,640]{1,0:T(8,128)(2,1)}) %reduce-scatter.71.cloned.1.call-update) | async-done | bytes 102416 | tf_op jit(solution)/shard_map/reduce_scatter | solution.py:256
  3406.9 78.6 %reduce-scatter.69.cloned.1.call-done = bf16[80,640]{1,0:T(8,128)(2,1)} async-done(((bf16[1280,640]{1,0:T(8,128)(2,1)}), bf16[80,640]{1,0:T(8,128)(2,1)}) %reduce-scatter.69.cloned.1.call-update) | async-done | bytes 102416 | tf_op jit(solution)/shard_map/reduce_scatter | solution.py:256
  3485.5 78.2 %reduce-scatter.67.cloned.1.call-done = bf16[80,640]{1,0:T(8,128)(2,1)} async-done(((bf16[1280,640]{1,0:T(8,128)(2,1)}), bf16[80,640]{1,0:T(8,128)(2,1)}) %reduce-scatter.67.cloned.1.call-update) | async-done | bytes 102416 | tf_op jit(solution)/shard_map/reduce_scatter | solution.py:256
  3563.7 78.5 %reduce-scatter.65.cloned.1.call-done = bf16[80,640]{1,0:T(8,128)(2,1)} async-done(((bf16[1280,640]{1,0:T(8,128)(2,1)}), bf16[80,640]{1,0:T(8,128)(2,1)}) %reduce-scatter.65.cloned.1.call-update) | async-done | bytes 102416 | tf_op jit(solution)/shard_map/reduce_scatter | solution.py:256
  (993 shorter events, 532.4 us)
Async XLA Ops:
  7.2 64.6 %all-gather.15.cloned.1.call-start = ((), (), s32[]{:S(2)}) async-start(), calls=%async_computation.32 | async-start | bytes 1740800 | tf_op jit(solution)/shard_map/all_gather | solution.py:58
  7.9 123.5 %all-gather.17.cloned.1.call-start = ((), (), s32[]{:S(2)}) async-start(), calls=%async_computation.33 | async-start | bytes 1740800 | tf_op jit(solution)/shard_map/all_gather | solution.py:59
  8.7 182.5 %all-gather.19.cloned.1.call-start = ((), (), s32[]{:S(2)}) async-start(), calls=%async_computation.34 | async-start | bytes 1740800 | tf_op jit(solution)/shard_map/all_gather | solution.py:60
  9.4 251.7 %all-gather.37.cloned.1.call-start = ((), (), s32[]{:S(2)}) async-start(), calls=%async_computation.43 | async-start | bytes 2785280 | tf_op jit(solution)/shard_map/all_gather | solution.py:85
  57.4 372.9 %copy-start.87 = (f32[1280]{0:T(1024)}, f32[1280]{0:T(1024)S(1)}, u32[]{:S(2)}) copy-start(f32[1280]{0:T(1024)S(1)} %convert_element_type.618) | copy-start | bytes 15364
  59.0 134.9 %copy-start.141 = (f32[128]{0:T(128)}, f32[128]{0:T(128)S(1)}, u32[]{:S(2)}) copy-start(f32[128]{0:T(128)S(1)} %get-tuple-element.980) | copy-start | bytes 1540
  198.1 129.1 %all-gather.35.cloned.1.call-start = ((), (), s32[]{:S(2)}) async-start(), calls=%async_computation.42 | async-start | bytes 2785280 | tf_op jit(solution)/shard_map/all_gather | solution.py:86
  198.7 188.2 %all-gather.25.cloned.1.call-start = ((), (), s32[]{:S(2)}) async-start(), calls=%async_computation.37 | async-start | bytes 1740800 | tf_op jit(solution)/shard_map/all_gather | solution.py:64
  199.3 207.7 %all-reduce.21.cloned.1.call-start = ((), (), s32[]{:S(2)}) async-start(), calls=%async_computation.44 | async-start | bytes 655360 | tf_op jit(solution)/shard_map/psum | solution.py:113
  202.4 63.1 %copy-start.61 = (f32[128,640]{0,1:T(8,128)}, f32[128,640]{0,1:T(8,128)S(1)}, u32[]{:S(2)}) copy-start(f32[128,640]{0,1:T(8,128)S(1)} %copy.178) | copy-start | bytes 983044
  202.6 129.2 %copy-start.14 = (bf16[128,8,80]{0,2,1:T(8,128)(2,1)}, bf16[128,8,80]{0,2,1:T(8,128)(2,1)S(1)}, u32[]{:S(2)}) copy-start(bf16[128,8,80]{0,2,1:T(8,128)(2,1)S(1)} %multiply_convert_fusion.11) | copy-start | bytes 491524
  340.3 68.1 %copy-start.89 = (bf16[128,8,80]{0,2,1:T(8,128)(2,1)}, bf16[128,8,80]{0,2,1:T(8,128)(2,1)S(1)}, u32[]{:S(2)}) copy-start(bf16[128,8,80]{0,2,1:T(8,128)(2,1)S(1)} %get-tuple-element.1002) | copy-start | bytes 491524
  389.7 79.7 %all-gather.27.cloned.1.call-start = ((), (), s32[]{:S(2)}) async-start(), calls=%async_computation.38 | async-start | bytes 1740800 | tf_op jit(solution)/shard_map/all_gather | solution.py:61
  390.4 139.1 %all-gather.29.cloned.1.call-start = ((), (), s32[]{:S(2)}) async-start(), calls=%async_computation.39 | async-start | bytes 1740800 | tf_op jit(solution)/shard_map/all_gather | solution.py:65
  391.1 204.7 %all-gather.41.cloned.1.call-start = ((), (), s32[]{:S(2)}) async-start(), calls=%async_computation.46 | async-start | bytes 2785280 | tf_op jit(solution)/shard_map/all_gather | solution.py:85
  413.0 249.4 %all-gather.23.cloned.1.call-start = ((), (), s32[]{:S(2)}) async-start(), calls=%async_computation.36 | async-start | bytes 2785280 | tf_op jit(solution)/shard_map/all_gather | solution.py:85
  428.4 300.6 %all-gather.39.cloned.1.call-start = ((), (), s32[]{:S(2)}) async-start(), calls=%async_computation.45 | async-start | bytes 2785280 | tf_op jit(solution)/shard_map/all_gather | solution.py:86
  428.9 366.6 %all-gather.21.cloned.1.call-start = ((), (), s32[]{:S(2)}) async-start(), calls=%async_computation.35 | async-start | bytes 2785280 | tf_op jit(solution)/shard_map/all_gather | solution.py:86
  429.7 432.3 %all-gather.33.cloned.1.call-start = ((), (), s32[]{:S(2)}) async-start(), calls=%async_computation.41 | async-start | bytes 2785280 | tf_op jit(solution)/shard_map/all_gather | solution.py:85
  435.4 493.0 %all-gather.31.cloned.1.call-start = ((), (), s32[]{:S(2)}) async-start(), calls=%async_computation.40 | async-start | bytes 2785280 | tf_op jit(solution)/shard_map/all_gather | solution.py:86
  438.7 524.4 %copy-start.154 = (f32[128]{0:T(128)}, f32[128]{0:T(128)S(1)}, u32[]{:S(2)}) copy-start(f32[128]{0:T(128)S(1)} %get-tuple-element.984) | copy-start | bytes 1540
  438.7 524.4 %all-reduce.27.cloned.1.call-start = ((), (), s32[]{:S(2)}) async-start(), calls=%async_computation.81 | async-start | bytes 2621440 | tf_op jit(solution)/shard_map/psum | solution.py:113
  438.9 227.9 %copy-start.20 = (bf16[128,8,80]{0,2,1:T(8,128)(2,1)}, bf16[128,8,80]{0,2,1:T(8,128)(2,1)S(1)}, u32[]{:S(2)}) copy-start(bf16[128,8,80]{0,2,1:T(8,128)(2,1)S(1)} %get-tuple-element.1438) | copy-start | bytes 491524
  438.9 427.5 %copy-start.17 = (bf16[128,8,80]{0,2,1:T(8,128)(2,1)}, bf16[128,8,80]{0,2,1:T(8,128)(2,1)S(1)}, u32[]{:S(2)}) copy-start(bf16[128,8,80]{0,2,1:T(8,128)(2,1)S(1)} %get-tuple-element.1486) | copy-start | bytes 491524
  533.4 66.8 %copy-start.72 = (pred[128,2048]{1,0:T(8,128)(4,1)S(1)}, pred[128,2048]{1,0:T(8,128)(4,1)}, u32[]{:S(2)}) copy-start(pred[128,2048]{1,0:T(8,128)(4,1)} %get-tuple-element.992) | copy-start | bytes 786436
  673.3 193.2 %copy-start.120 = (f32[8,128]{1,0:T(8,128)}, f32[8,128]{1,0:T(8,128)S(1)}, u32[]{:S(2)}) copy-start(f32[8,128]{1,0:T(8,128)S(1)} %get-tuple-element.1012) | copy-start | bytes 12292
  800.0 66.4 %copy-start.69 = (pred[128,2048]{1,0:T(8,128)(4,1)S(1)}, pred[128,2048]{1,0:T(8,128)(4,1)}, u32[]{:S(2)}) copy-start(pred[128,2048]{1,0:T(8,128)(4,1)} %get-tuple-element.991) | copy-start | bytes 786436
  943.9 51.4 %all-reduce.25.cloned.1.call-start = ((), (), s32[]{:S(2)}) async-start(), calls=%async_computation.80 | async-start | bytes 1966080 | tf_op jit(solution)/shard_map/psum | solution.py:133
  974.3 387.5 %reduce-scatter.47.cloned.1.call-start = ((), (), s32[]{:S(2)}) async-start(), calls=%async_computation.54 | async-start | bytes 2785280 | tf_op jit(solution)/shard_map/reduce_scatter | solution.py:210
  1076.8 285.0 %reduce-scatter.45.cloned.1.call-start = ((), (), s32[]{:S(2)}) async-start(), calls=%async_computation.53 | async-start | bytes 2785280 | tf_op jit(solution)/shard_map/reduce_scatter | solution.py:204
  1082.9 283.7 %reduce-scatter.35.cloned.1.call-start = ((), (), s32[]{:S(2)}) async-start(), calls=%async_computation.48 | async-start | bytes 2785280 | tf_op jit(solution)/shard_map/reduce_scatter | solution.py:210
  1159.0 247.3 %reduce-scatter.33.cloned.1.call-start = ((), (), s32[]{:S(2)}) async-start(), calls=%async_computation.47 | async-start | bytes 2785280 | tf_op jit(solution)/shard_map/reduce_scatter | solution.py:204
  1161.8 325.8 %reduce-scatter.39.cloned.1.call-start = ((), (), s32[]{:S(2)}) async-start(), calls=%async_computation.50 | async-start | bytes 2785280 | tf_op jit(solution)/shard_map/reduce_scatter | solution.py:210
  1237.9 332.0 %reduce-scatter.37.cloned.1.call-start = ((), (), s32[]{:S(2)}) async-start(), calls=%async_computation.49 | async-start | bytes 2785280 | tf_op jit(solution)/shard_map/reduce_scatter | solution.py:204
  1240.7 410.9 %reduce-scatter.43.cloned.1.call-start = ((), (), s32[]{:S(2)}) async-start(), calls=%async_computation.52 | async-start | bytes 2785280 | tf_op jit(solution)/shard_map/reduce_scatter | solution.py:210
  1316.0 417.4 %reduce-scatter.41.cloned.1.call-start = ((), (), s32[]{:S(2)}) async-start(), calls=%async_computation.51 | async-start | bytes 2785280 | tf_op jit(solution)/shard_map/reduce_scatter | solution.py:204
  1316.8 495.5 %reduce-scatter.85.cloned.1.call-start = ((), (), s32[]{:S(2)}) async-start(), calls=%async_computation.73 | async-start | bytes 1740800 | tf_op jit(solution)/shard_map/reduce_scatter | solution.py:259
  1319.4 571.2 %reduce-scatter.87.cloned.1.call-start = ((), (), s32[]{:S(2)}) async-start(), calls=%async_computation.74 | async-start | bytes 1740800 | tf_op jit(solution)/shard_map/reduce_scatter | solution.py:259
  1321.4 647.5 %reduce-scatter.83.cloned.1.call-start = ((), (), s32[]{:S(2)}) async-start(), calls=%async_computation.72 | async-start | bytes 1740800 | tf_op jit(solution)/shard_map/reduce_scatter | solution.py:259
  1323.4 724.0 %reduce-scatter.81.cloned.1.call-start = ((), (), s32[]{:S(2)}) async-start(), calls=%async_computation.71 | async-start | bytes 1740800 | tf_op jit(solution)/shard_map/reduce_scatter | solution.py:259
  1325.8 800.1 %reduce-scatter.93.cloned.1.call-start = ((), (), s32[]{:S(2)}) async-start(), calls=%async_computation.77 | async-start | bytes 1740800 | tf_op jit(solution)/shard_map/reduce_scatter | solution.py:271
  1328.7 875.5 %reduce-scatter.95.cloned.1.call-start = ((), (), s32[]{:S(2)}) async-start(), calls=%async_computation.78 | async-start | bytes 1740800 | tf_op jit(solution)/shard_map/reduce_scatter | solution.py:271
  1331.6 951.1 %reduce-scatter.91.cloned.1.call-start = ((), (), s32[]{:S(2)}) async-start(), calls=%async_computation.76 | async-start | bytes 1740800 | tf_op jit(solution)/shard_map/reduce_scatter | solution.py:271
  1334.5 1026.4 %reduce-scatter.89.cloned.1.call-start = ((), (), s32[]{:S(2)}) async-start(), calls=%async_computation.75 | async-start | bytes 1740800 | tf_op jit(solution)/shard_map/reduce_scatter | solution.py:271
  1337.5 1101.6 %reduce-scatter.79.cloned.1.call-start = ((), (), s32[]{:S(2)}) async-start(), calls=%async_computation.70 | async-start | bytes 1740800 | tf_op jit(solution)/shard_map/reduce_scatter | solution.py:268
  1340.5 1177.1 %reduce-scatter.77.cloned.1.call-start = ((), (), s32[]{:S(2)}) async-start(), calls=%async_computation.69 | async-start | bytes 1740800 | tf_op jit(solution)/shard_map/reduce_scatter | solution.py:268
  1343.5 1252.5 %reduce-scatter.75.cloned.1.call-start = ((), (), s32[]{:S(2)}) async-start(), calls=%async_computation.68 | async-start | bytes 1740800 | tf_op jit(solution)/shard_map/reduce_scatter | solution.py:268
  1346.3 1328.1 %reduce-scatter.73.cloned.1.call-start = ((), (), s32[]{:S(2)}) async-start(), calls=%async_computation.67 | async-start | bytes 1740800 | tf_op jit(solution)/shard_map/reduce_scatter | solution.py:268
  1351.0 1346.1 %all-reduce.23.cloned.1.call-start = ((), (), s32[]{:S(2)}) async-start(), calls=%async_computation.79 | async-start | bytes 5242880 | tf_op jit(solution)/shard_map/psum | solution.py:122
  1738.3 1046.4 %reduce-scatter.55.cloned.1.call-start = ((), (), s32[]{:S(2)}) async-start(), calls=%async_computation.58 | async-start | bytes 1740800 | tf_op jit(solution)/shard_map/reduce_scatter | solution.py:250
  1743.2 1115.3 %reduce-scatter.53.cloned.1.call-start = ((), (), s32[]{:S(2)}) async-start(), calls=%async_computation.57 | async-start | bytes 1740800 | tf_op jit(solution)/shard_map/reduce_scatter | solution.py:250
  1747.4 1189.4 %reduce-scatter.51.cloned.1.call-start = ((), (), s32[]{:S(2)}) async-start(), calls=%async_computation.56 | async-start | bytes 1740800 | tf_op jit(solution)/shard_map/reduce_scatter | solution.py:250
  1751.4 1263.9 %reduce-scatter.49.cloned.1.call-start = ((), (), s32[]{:S(2)}) async-start(), calls=%async_computation.55 | async-start | bytes 1740800 | tf_op jit(solution)/shard_map/reduce_scatter | solution.py:250
  1755.4 1338.4 %reduce-scatter.63.cloned.1.call-start = ((), (), s32[]{:S(2)}) async-start(), calls=%async_computation.62 | async-start | bytes 1740800 | tf_op jit(solution)/shard_map/reduce_scatter | solution.py:253
  1756.0 1416.2 %reduce-scatter.61.cloned.1.call-start = ((), (), s32[]{:S(2)}) async-start(), calls=%async_computation.61 | async-start | bytes 1740800 | tf_op jit(solution)/shard_map/reduce_scatter | solution.py:253
  1756.8 1493.8 %reduce-scatter.59.cloned.1.call-start = ((), (), s32[]{:S(2)}) async-start(), calls=%async_computation.60 | async-start | bytes 1740800 | tf_op jit(solution)/shard_map/reduce_scatter | solution.py:253
  1757.3 1571.6 %reduce-scatter.57.cloned.1.call-start = ((), (), s32[]{:S(2)}) async-start(), calls=%async_computation.59 | async-start | bytes 1740800 | tf_op jit(solution)/shard_map/reduce_scatter | solution.py:253
  1757.9 1649.0 %reduce-scatter.71.cloned.1.call-start = ((), (), s32[]{:S(2)}) async-start(), calls=%async_computation.66 | async-start | bytes 1740800 | tf_op jit(solution)/shard_map/reduce_scatter | solution.py:256
  1758.5 1727.0 %reduce-scatter.69.cloned.1.call-start = ((), (), s32[]{:S(2)}) async-start(), calls=%async_computation.65 | async-start | bytes 1740800 | tf_op jit(solution)/shard_map/reduce_scatter | solution.py:256
  1759.1 1804.6 %reduce-scatter.67.cloned.1.call-start = ((), (), s32[]{:S(2)}) async-start(), calls=%async_computation.64 | async-start | bytes 1740800 | tf_op jit(solution)/shard_map/reduce_scatter | solution.py:256
  1759.7 1882.5 %reduce-scatter.65.cloned.1.call-start = ((), (), s32[]{:S(2)}) async-start(), calls=%async_computation.63 | async-start | bytes 1740800 | tf_op jit(solution)/shard_map/reduce_scatter | solution.py:256
  2676.1 101.9 %copy-start.47 = (bf16[128,1280]{1,0:T(8,128)(2,1)S(1)}, bf16[128,1280]{1,0:T(8,128)(2,1)}, u32[]{:S(2)}) copy-start(bf16[128,1280]{1,0:T(8,128)(2,1)} %all-reduce.21.cloned.1.call-done) | copy-start | bytes 983044
  2676.2 101.9 %copy-start.50 = (f32[128,1280]{1,0:T(8,128)S(1)}, f32[128,1280]{1,0:T(8,128)}, u32[]{:S(2)}) copy-start(f32[128,1280]{1,0:T(8,128)} %copy-done.48) | copy-start | bytes 1966084
  2676.2 101.9 %copy-start.157 = (f32[128]{0:T(128)S(1)}, f32[128]{0:T(128)}, u32[]{:S(2)}) copy-start(f32[128]{0:T(128)} %get-tuple-element.981) | copy-start | bytes 1540
  (208 other events, 1070.1 us)
Sparse Core Ops, SparseCore 0:
  10.7 61.0 all-gather.14
  74.4 56.9 all-gather.16
  134.1 56.9 all-gather.18
  198.2 62.8 all-gather.36
  264.3 62.9 all-gather.34
  329.8 57.0 all-gather.24
  389.8 17.2 all-reduce.20
  410.1 59.2 all-gather.26
  472.5 56.9 all-gather.28
  532.9 62.8 all-gather.40
  599.4 62.9 all-gather.22
  665.9 62.9 all-gather.38
  732.5 62.9 all-gather.20
  799.0 62.9 all-gather.32
  865.5 62.9 all-gather.30
  944.0 19.0 all-reduce.26
  974.4 20.8 all-reduce.24
  1076.9 83.4 reduce-scatter.46
  1163.4 79.0 reduce-scatter.44
  1244.8 79.4 reduce-scatter.34
  1326.7 79.6 reduce-scatter.32
  1408.7 78.8 reduce-scatter.38
  1490.0 79.7 reduce-scatter.36
  1572.1 79.4 reduce-scatter.42
  1653.9 79.4 reduce-scatter.40
  1735.7 76.5 reduce-scatter.84
  1814.4 76.1 reduce-scatter.86
  1893.0 75.8 reduce-scatter.82
  1971.2 76.1 reduce-scatter.80
  2049.6 76.2 reduce-scatter.92
  2128.2 76.0 reduce-scatter.94
  2206.6 76.0 reduce-scatter.90
  2284.8 76.0 reduce-scatter.88
  2363.3 75.7 reduce-scatter.78
  2441.4 76.1 reduce-scatter.76
  2519.8 76.0 reduce-scatter.74
  2598.1 76.2 reduce-scatter.72
  2678.0 19.0 all-reduce.22
  2699.2 80.8 reduce-scatter.54
  2782.5 75.9 reduce-scatter.52
  2860.9 75.8 reduce-scatter.50
  2939.2 76.0 reduce-scatter.48
  3017.4 76.3 reduce-scatter.62
  3096.2 76.0 reduce-scatter.60
  3174.4 76.1 reduce-scatter.58
  3252.8 76.0 reduce-scatter.56
  3331.1 75.7 reduce-scatter.70
  3409.1 76.3 reduce-scatter.68
  3487.7 75.9 reduce-scatter.66
  3566.1 76.0 reduce-scatter.64
where the time goes:
time: 3670 us; the launch traced here: 3650 us
  waiting for transfers between devices  2880 us (78%)
  matrix products  254 us (7%)
  local copies, waits for them, and re-layouts  219 us (6%)
  blocking collectives  163 us (4%)
  other arithmetic  99 us (3%)
    reduce_scatter x4, waiting for transfers between devices, per_device(): lax.psum_scatter(grads[1].astype(jnp.bfloat16), 'ctx', scatter_dimension=...  312 us
    reduce_scatter x4, waiting for transfers between devices, per_device(): lax.psum_scatter(grads[7].astype(jnp.bfloat16), 'ctx', scatter_dimension=...  312 us
    reduce_scatter x4, waiting for transfers between devices, per_device(): lax.psum_scatter(grads[6].astype(jnp.bfloat16), 'ctx', scatter_dimension=...  312 us
    reduce_scatter x4, waiting for transfers between devices, per_device(): lax.psum_scatter(grads[2].astype(jnp.bfloat16), 'ctx', scatter_dimension=...  311 us
    reduce_scatter x4, waiting for transfers between devices, per_device(): lax.psum_scatter(grads[3].astype(jnp.bfloat16), 'ctx', scatter_dimension=...  246 us
    all_gather x4, waiting for transfers between devices, per_device(): key_piece = lax.all_gather(key_local, 'ctx', axis=0, tiled=True)  239 us
    reduce_scatter x4, waiting for transfers between devices, per_device(): lax.psum_scatter(grads[0].astype(jnp.bfloat16), 'ctx', scatter_dimension=...  231 us
    all_gather x4, waiting for transfers between devices, per_device(): value_piece = lax.all_gather(value_local, 'ctx', axis=0, tiled=True)  217 us
  transfers between devices with their start and end apart: 50, of which 46 were waited for; matrix products, arithmetic and copies ran while one was open for 12% of the time, Pallas kernels for 0%

commit v1 on v0

--- a/solution.py
+++ b/solution.py
@@ -82,8 +82,13 @@
         key_local = projected[:, local_cols : 2 * local_cols].astype(jnp.bfloat16)
         value_local = projected[:, 2 * local_cols :].astype(jnp.bfloat16)
         row_top = jnp.full((head_count, tok_rows), MASKED, jnp.float32)
-        key_piece = lax.all_gather(key_local, "ctx", axis=0, tiled=True)
-        value_piece = lax.all_gather(value_local, "ctx", axis=0, tiled=True)
+        key_piece, value_piece = jnp.split(
+            lax.all_gather(
+                jnp.concatenate([key_local, value_local], axis=1), "ctx", axis=0, tiled=True
+            ),
+            [key_local.shape[1]],
+            axis=1,
+        )
         length = key_piece.shape[0]
         key_pos = jnp.arange(length, dtype=jnp.int32)
         allowed = (key_pos[None, :] <= positions[:, None]) & (

time: 3670 us -> 3960 us (1.079)
  waiting for transfers between devices: 2880 us -> 3170 us
    all_gather x8 -> x12, waiting for transfers between devices: 456 us -> 589 us  [the longest x4 297 us: per_device(): lax.all_gather(jnp.concatenate([key_local, value_local], axis=1), 'ctx',...]
    reduce_scatter x4, waiting for transfers between devices: 204 us -> 290 us  [per_device(): lax.psum_scatter(key_terms.reshape(stream, local_cols).astype(jnp.bfloat1...]
    reduce_scatter x4, waiting for transfers between devices: 153 us -> 231 us  [per_device(): lax.psum_scatter(value_terms.reshape(stream, local_cols).astype(jnp.bfloa...]
    split x0 -> x12, local copies, waits for them, and re-layouts: none -> 57 us  [per_device(): jnp.split(lax.all_gather(jnp.concatenate([key_local, value_local], axis=1...]
  transfers between devices with their start and end apart: 50 -> 54, of which waited for: 46 -> 49; matrix products, arithmetic and copies ran while one was open for 12% -> 13% of each run, Pallas kernels for 0% -> 0%
where the time goes in v1:
time: 3960 us; the launch traced here: 3950 us
  waiting for transfers between devices  3170 us (80%)
  matrix products  258 us (7%)
  local copies, waits for them, and re-layouts  248 us (6%)
  blocking collectives  162 us (4%)
  other arithmetic  88.9 us (2%)
    reduce_scatter x4, waiting for transfers between devices, per_device(): lax.psum_scatter(grads[6].astype(jnp.bfloat16), 'ctx', scatter_dimension=...  312 us
    reduce_scatter x4, waiting for transfers between devices, per_device(): lax.psum_scatter(grads[7].astype(jnp.bfloat16), 'ctx', scatter_dimension=...  312 us
    reduce_scatter x4, waiting for transfers between devices, per_device(): lax.psum_scatter(grads[1].astype(jnp.bfloat16), 'ctx', scatter_dimension=...  311 us
    reduce_scatter x4, waiting for transfers between devices, per_device(): lax.psum_scatter(grads[2].astype(jnp.bfloat16), 'ctx', scatter_dimension=...  311 us
    all_gather x4, waiting for transfers between devices, per_device(): lax.all_gather(jnp.concatenate([key_local, value_local], axis=1), 'ctx',...  297 us
    reduce_scatter x4, waiting for transfers between devices, per_device(): lax.psum_scatter(key_terms.reshape(stream, local_cols).astype(jnp.bfloat1...  290 us
    reduce_scatter x4, waiting for transfers between devices, per_device(): lax.psum_scatter(grads[3].astype(jnp.bfloat16), 'ctx', scatter_dimension=...  245 us
    reduce_scatter x4, waiting for transfers between devices, per_device(): lax.psum_scatter(value_terms.reshape(stream, local_cols).astype(jnp.bfloa...  231 us
  transfers between devices with their start and end apart: 54, of which 49 were waited for; matrix products, arithmetic and copies ran while one was open for 13% of the time, Pallas kernels for 0%

profile of v1, /device:TPU:0, one launch (start us, length us, event | category | flops | bytes accessed | tf_op | source)
XLA Modules:
  0.0 3948.8 jit_solution(11535970523160682145)
XLA Ops:
  13.1 44.2 %all-reduce.11 = (bf16[1280]{0:T(1024)(128)(2,1)S(1)}, bf16[1280]{0:T(1024)(128)(2,1)S(1)}) all-reduce(bf16[1280]{0:T(1024)(128)(2,1)S(1)} %dynamic-update-slice, bf16[1280]{0:T(1024)(128)(2,1)S(1)} %dynamic-update-slice.1), channel_id=1, replica_groups=mesh['ctx'=16,'tp'=2] {'ctx'}, use_global_device_ids=true, to_apply=%add | all-reduce | flops 2560 | bytes 10240
  59.1 12.6 all-gather.19.cloned.1.call-done
  74.6 56.8 %all-gather.21.cloned.1.call-done = bf16[1280,640]{1,0:T(8,128)(2,1)} async-done(((bf16[80,640]{1,0:T(8,128)(2,1)}), bf16[1280,640]{1,0:T(8,128)(2,1)}) %all-gather.21.cloned.1.call-update) | async-done | bytes 1638416 | tf_op jit(solution)/shard_map/all_gather | solution.py:59
  134.2 56.9 %all-gather.23.cloned.1.call-done = bf16[1280,640]{1,0:T(8,128)(2,1)} async-done(((bf16[80,640]{1,0:T(8,128)(2,1)}), bf16[1280,640]{1,0:T(8,128)(2,1)}) %all-gather.23.cloned.1.call-update) | async-done | bytes 1638416 | tf_op jit(solution)/shard_map/all_gather | solution.py:60
  202.8 80.4 %all-gather.35.cloned.1.call-done = bf16[2048,1280]{1,0:T(8,128)(2,1)} async-done(((bf16[128,1280]{1,0:T(8,128)(2,1)}), bf16[2048,1280]{1,0:T(8,128)(2,1)}) %all-gather.35.cloned.1.call-update) | async-done | bytes 5242896 | tf_op jit(solution)/shard_map/all_gather | solution.py:86
  283.1 5.3 fusion.257
  305.9 36.5 all-gather.27.cloned.1.call-done
  346.7 15.8 all-reduce.21.cloned.1.call-done
  385.5 39.4 all-gather.29.cloned.1.call-done
  427.8 57.2 %all-gather.31.cloned.1.call-done = bf16[640,1280]{0,1:T(8,128)(2,1)} async-done(((bf16[640,80]{0,1:T(8,128)(2,1)}), bf16[640,1280]{0,1:T(8,128)(2,1)}) %all-gather.31.cloned.1.call-update) | async-done | bytes 1638416 | tf_op jit(solution)/shard_map/all_gather | solution.py:65
  489.0 83.2 %all-gather.37.cloned.1.call-done = bf16[2048,1280]{1,0:T(8,128)(2,1)} async-done(((bf16[128,1280]{1,0:T(8,128)(2,1)}), bf16[2048,1280]{1,0:T(8,128)(2,1)}) %all-gather.37.cloned.1.call-update) | async-done | bytes 5242896 | tf_op jit(solution)/shard_map/all_gather | solution.py:86
  572.2 5.4 fusion.256
  586.4 72.5 %all-gather.25.cloned.1.call-done = bf16[2048,1280]{1,0:T(8,128)(2,1)} async-done(((bf16[128,1280]{1,0:T(8,128)(2,1)}), bf16[2048,1280]{1,0:T(8,128)(2,1)}) %all-gather.25.cloned.1.call-update) | async-done | bytes 5242896 | tf_op jit(solution)/shard_map/all_gather | solution.py:86
  658.9 5.3 fusion.255
  673.2 6.6 select_reduce_fusion
  684.6 61.2 %all-gather.33.cloned.1.call-done = bf16[2048,1280]{1,0:T(8,128)(2,1)} async-done(((bf16[128,1280]{1,0:T(8,128)(2,1)}), bf16[2048,1280]{1,0:T(8,128)(2,1)}) %all-gather.33.cloned.1.call-update) | async-done | bytes 5242896 | tf_op jit(solution)/shard_map/all_gather | solution.py:86
  745.8 5.2 fusion.254
  755.6 6.5 select_reduce_fusion.2
  771.3 6.3 fusion.270
  792.4 18.8 all-reduce.27.cloned.1.call-done
  832.6 10.2 all-reduce.25.cloned.1.call-done
  850.1 61.4 %all-gather.51.cloned.1.call-done = bf16[2048,640]{1,0:T(8,128)(2,1)} async-done(((bf16[128,640]{1,0:T(8,128)(2,1)}), bf16[2048,640]{1,0:T(8,128)(2,1)}) %all-gather.51.cloned.1.call-update) | async-done | bytes 2621456 | tf_op jit(solution)/shard_map/all_gather | solution.py:157
  911.6 66.5 %all-gather.53.cloned.1.call-done = bf16[2048,640]{1,0:T(8,128)(2,1)} async-done(((bf16[128,640]{1,0:T(8,128)(2,1)}), bf16[2048,640]{1,0:T(8,128)(2,1)}) %all-gather.53.cloned.1.call-update) | async-done | bytes 2621456 | tf_op jit(solution)/shard_map/all_gather | solution.py:158
  981.4 65.3 %while.63 = (s32[]{:T(128)}, f32[128,8,80]{0,2,1:T(8,128)}, bf16[4,512,640]{2,1,0:T(8,128)(2,1)}, bf16[4,512,640]{2,1,0:T(8,128)(2,1)}, bf16[4,512,640]{2,1,0:T(...) while((s32[]{:T(128)}, f32[128,8,80]{0,2,1:T(8,128)}, ...), condition=%wide.region_67.68_spmd.clone, body=%wide.region_65.67_spmd.clone.sunk | while | flops 423997568 | bytes 28663612 | solution.py:207
  1054.0 57.0 %all-gather.41.cloned.1.call-done = bf16[2048,640]{1,0:T(8,128)(2,1)} async-done(((bf16[128,640]{1,0:T(8,128)(2,1)}), bf16[2048,640]{1,0:T(8,128)(2,1)}) %all-gather.41.cloned.1.call-update) | async-done | bytes 2621456 | tf_op jit(solution)/shard_map/all_gather | solution.py:158
  1114.5 71.6 %while.60 = (s32[]{:T(128)}, f32[128,8,80]{0,2,1:T(8,128)}, bf16[4,512,640]{2,1,0:T(8,128)(2,1)}, bf16[4,512,640]{2,1,0:T(8,128)(2,1)}, bf16[4,512,640]{2,1,0:T(...) while((s32[]{:T(128)}, f32[128,8,80]{0,2,1:T(8,128)}, ...), condition=%wide.region_40.41_spmd.clone, body=%wide.region_38.40_spmd.clone.sunk | while | flops 423997568 | bytes 30629728 | solution.py:207
  1190.0 52.9 %all-gather.45.cloned.1.call-done = bf16[2048,640]{1,0:T(8,128)(2,1)} async-done(((bf16[128,640]{1,0:T(8,128)(2,1)}), bf16[2048,640]{1,0:T(8,128)(2,1)}) %all-gather.45.cloned.1.call-update) | async-done | bytes 2621456 | tf_op jit(solution)/shard_map/all_gather | solution.py:158
  1246.4 71.0 %while.61 = (s32[]{:T(128)}, f32[128,8,80]{0,2,1:T(8,128)}, bf16[4,512,640]{2,1,0:T(8,128)(2,1)}, bf16[4,512,640]{2,1,0:T(8,128)(2,1)}, bf16[4,512,640]{2,1,0:T(...) while((s32[]{:T(128)}, f32[128,8,80]{0,2,1:T(8,128)}, ...), condition=%wide.region_49.50_spmd.clone, body=%wide.region_47.49_spmd.clone.sunk | while | flops 423997568 | bytes 30629728 | solution.py:207
  1321.3 53.6 %all-gather.49.cloned.1.call-done = bf16[2048,640]{1,0:T(8,128)(2,1)} async-done(((bf16[128,640]{1,0:T(8,128)(2,1)}), bf16[2048,640]{1,0:T(8,128)(2,1)}) %all-gather.49.cloned.1.call-update) | async-done | bytes 2621456 | tf_op jit(solution)/shard_map/all_gather | solution.py:158
  1378.3 71.6 %while.62 = (s32[]{:T(128)}, f32[128,8,80]{0,2,1:T(8,128)}, bf16[4,512,640]{2,1,0:T(8,128)(2,1)}, bf16[4,512,640]{2,1,0:T(8,128)(2,1)}, bf16[4,512,640]{2,1,0:T(...) while((s32[]{:T(128)}, f32[128,8,80]{0,2,1:T(8,128)}, ...), condition=%wide.region_58.59_spmd.clone, body=%wide.region_56.58_spmd.clone.sunk | while | flops 423997568 | bytes 30629728 | solution.py:207
  1496.2 44.5 %reduce-scatter.45.cloned.1.call-done = bf16[128,640]{1,0:T(8,128)(2,1)} async-done(((bf16[2048,640]{1,0:T(8,128)(2,1)}), bf16[128,640]{1,0:T(8,128)(2,1)}) %reduce-scatter.45.cloned.1.call-update) | async-done | bytes 163856 | tf_op jit(solution)/shard_map/reduce_scatter | solution.py:209
  1540.7 4.9 convolution_convert_fusion.16
  1545.6 77.1 %reduce-scatter.35.cloned.1.call-done = bf16[128,640]{1,0:T(8,128)(2,1)} async-done(((bf16[2048,640]{1,0:T(8,128)(2,1)}), bf16[128,640]{1,0:T(8,128)(2,1)}) %reduce-scatter.35.cloned.1.call-update) | async-done | bytes 163856 | tf_op jit(solution)/shard_map/reduce_scatter | solution.py:215
  1622.7 82.1 %reduce-scatter.33.cloned.1.call-done = bf16[128,640]{1,0:T(8,128)(2,1)} async-done(((bf16[2048,640]{1,0:T(8,128)(2,1)}), bf16[128,640]{1,0:T(8,128)(2,1)}) %reduce-scatter.33.cloned.1.call-update) | async-done | bytes 163856 | tf_op jit(solution)/shard_map/reduce_scatter | solution.py:209
  1709.5 76.8 %reduce-scatter.39.cloned.1.call-done = bf16[128,640]{1,0:T(8,128)(2,1)} async-done(((bf16[2048,640]{1,0:T(8,128)(2,1)}), bf16[128,640]{1,0:T(8,128)(2,1)}) %reduce-scatter.39.cloned.1.call-update) | async-done | bytes 163856 | tf_op jit(solution)/shard_map/reduce_scatter | solution.py:215
  1786.3 81.5 %reduce-scatter.37.cloned.1.call-done = bf16[128,640]{1,0:T(8,128)(2,1)} async-done(((bf16[2048,640]{1,0:T(8,128)(2,1)}), bf16[128,640]{1,0:T(8,128)(2,1)}) %reduce-scatter.37.cloned.1.call-update) | async-done | bytes 163856 | tf_op jit(solution)/shard_map/reduce_scatter | solution.py:209
  1872.7 77.2 %reduce-scatter.43.cloned.1.call-done = bf16[128,640]{1,0:T(8,128)(2,1)} async-done(((bf16[2048,640]{1,0:T(8,128)(2,1)}), bf16[128,640]{1,0:T(8,128)(2,1)}) %reduce-scatter.43.cloned.1.call-update) | async-done | bytes 163856 | tf_op jit(solution)/shard_map/reduce_scatter | solution.py:215
  1949.8 82.0 %reduce-scatter.41.cloned.1.call-done = bf16[128,640]{1,0:T(8,128)(2,1)} async-done(((bf16[2048,640]{1,0:T(8,128)(2,1)}), bf16[128,640]{1,0:T(8,128)(2,1)}) %reduce-scatter.41.cloned.1.call-update) | async-done | bytes 163856 | tf_op jit(solution)/shard_map/reduce_scatter | solution.py:209
  2061.9 38.2 psum.167
  2100.1 10.4 reduce-scatter.85.cloned.1.call-done
  2110.4 78.4 %reduce-scatter.87.cloned.1.call-done = bf16[80,640]{1,0:T(8,128)(2,1)} async-done(((bf16[1280,640]{1,0:T(8,128)(2,1)}), bf16[80,640]{1,0:T(8,128)(2,1)}) %reduce-scatter.87.cloned.1.call-update) | async-done | bytes 102416 | tf_op jit(solution)/shard_map/reduce_scatter | solution.py:264
  2188.9 78.4 %reduce-scatter.83.cloned.1.call-done = bf16[80,640]{1,0:T(8,128)(2,1)} async-done(((bf16[1280,640]{1,0:T(8,128)(2,1)}), bf16[80,640]{1,0:T(8,128)(2,1)}) %reduce-scatter.83.cloned.1.call-update) | async-done | bytes 102416 | tf_op jit(solution)/shard_map/reduce_scatter | solution.py:264
  2267.2 78.3 %reduce-scatter.81.cloned.1.call-done = bf16[80,640]{1,0:T(8,128)(2,1)} async-done(((bf16[1280,640]{1,0:T(8,128)(2,1)}), bf16[80,640]{1,0:T(8,128)(2,1)}) %reduce-scatter.81.cloned.1.call-update) | async-done | bytes 102416 | tf_op jit(solution)/shard_map/reduce_scatter | solution.py:264
  2347.3 76.6 %reduce-scatter.93.cloned.1.call-done = bf16[640,80]{0,1:T(8,128)(2,1)} async-done(((bf16[640,1280]{0,1:T(8,128)(2,1)}), bf16[640,80]{0,1:T(8,128)(2,1)}) %reduce-scatter.93.cloned.1.call-update) | async-done | bytes 102416 | tf_op jit(solution)/shard_map/reduce_scatter | solution.py:276
  2423.9 78.4 %reduce-scatter.95.cloned.1.call-done = bf16[640,80]{0,1:T(8,128)(2,1)} async-done(((bf16[640,1280]{0,1:T(8,128)(2,1)}), bf16[640,80]{0,1:T(8,128)(2,1)}) %reduce-scatter.95.cloned.1.call-update) | async-done | bytes 102416 | tf_op jit(solution)/shard_map/reduce_scatter | solution.py:276
  2502.3 78.3 %reduce-scatter.91.cloned.1.call-done = bf16[640,80]{0,1:T(8,128)(2,1)} async-done(((bf16[640,1280]{0,1:T(8,128)(2,1)}), bf16[640,80]{0,1:T(8,128)(2,1)}) %reduce-scatter.91.cloned.1.call-update) | async-done | bytes 102416 | tf_op jit(solution)/shard_map/reduce_scatter | solution.py:276
  2580.6 78.4 %reduce-scatter.89.cloned.1.call-done = bf16[640,80]{0,1:T(8,128)(2,1)} async-done(((bf16[640,1280]{0,1:T(8,128)(2,1)}), bf16[640,80]{0,1:T(8,128)(2,1)}) %reduce-scatter.89.cloned.1.call-update) | async-done | bytes 102416 | tf_op jit(solution)/shard_map/reduce_scatter | solution.py:276
  2660.8 76.6 %reduce-scatter.79.cloned.1.call-done = bf16[640,80]{0,1:T(8,128)(2,1)} async-done(((bf16[640,1280]{0,1:T(8,128)(2,1)}), bf16[640,80]{0,1:T(8,128)(2,1)}) %reduce-scatter.79.cloned.1.call-update) | async-done | bytes 102416 | tf_op jit(solution)/shard_map/reduce_scatter | solution.py:273
  2737.4 78.3 %reduce-scatter.77.cloned.1.call-done = bf16[640,80]{0,1:T(8,128)(2,1)} async-done(((bf16[640,1280]{0,1:T(8,128)(2,1)}), bf16[640,80]{0,1:T(8,128)(2,1)}) %reduce-scatter.77.cloned.1.call-update) | async-done | bytes 102416 | tf_op jit(solution)/shard_map/reduce_scatter | solution.py:273
  2815.6 78.5 %reduce-scatter.75.cloned.1.call-done = bf16[640,80]{0,1:T(8,128)(2,1)} async-done(((bf16[640,1280]{0,1:T(8,128)(2,1)}), bf16[640,80]{0,1:T(8,128)(2,1)}) %reduce-scatter.75.cloned.1.call-update) | async-done | bytes 102416 | tf_op jit(solution)/shard_map/reduce_scatter | solution.py:273
  2894.1 78.4 %reduce-scatter.73.cloned.1.call-done = bf16[640,80]{0,1:T(8,128)(2,1)} async-done(((bf16[640,1280]{0,1:T(8,128)(2,1)}), bf16[640,80]{0,1:T(8,128)(2,1)}) %reduce-scatter.73.cloned.1.call-update) | async-done | bytes 102416 | tf_op jit(solution)/shard_map/reduce_scatter | solution.py:273
  2974.4 21.0 all-reduce.23.cloned.1.call-done
  2997.5 77.3 %all-reduce.10 = (bf16[1280]{0:T(1024)(128)(2,1)S(1)}, bf16[1280]{0:T(1024)(128)(2,1)S(1)}, bf16[1280]{0:T(1024)(128)(2,1)S(1)}, bf16[1280]{0:T(1024)(128)(2,1)S...) all-reduce(bf16[1280]{0:T(1024)(128)(2,1)S(1)} %get-tuple-element.7, ...), channel_id=37, replica_groups=mesh['ctx'=16,'tp'=2] {'ctx'}, use_global_device_ids=true, to_apply=%region_103.104.clone | all-reduce | flops 10240 | bytes 40960
  3082.6 74.1 %reduce-scatter.53.cloned.1.call-done = bf16[80,640]{1,0:T(8,128)(2,1)} async-done(((bf16[1280,640]{1,0:T(8,128)(2,1)}), bf16[80,640]{1,0:T(8,128)(2,1)}) %reduce-scatter.53.cloned.1.call-update) | async-done | bytes 102416 | tf_op jit(solution)/shard_map/reduce_scatter | solution.py:255
  3156.7 78.2 %reduce-scatter.51.cloned.1.call-done = bf16[80,640]{1,0:T(8,128)(2,1)} async-done(((bf16[1280,640]{1,0:T(8,128)(2,1)}), bf16[80,640]{1,0:T(8,128)(2,1)}) %reduce-scatter.51.cloned.1.call-update) | async-done | bytes 102416 | tf_op jit(solution)/shard_map/reduce_scatter | solution.py:255
  3234.9 78.5 %reduce-scatter.49.cloned.1.call-done = bf16[80,640]{1,0:T(8,128)(2,1)} async-done(((bf16[1280,640]{1,0:T(8,128)(2,1)}), bf16[80,640]{1,0:T(8,128)(2,1)}) %reduce-scatter.49.cloned.1.call-update) | async-done | bytes 102416 | tf_op jit(solution)/shard_map/reduce_scatter | solution.py:255
  3315.2 76.4 %reduce-scatter.63.cloned.1.call-done = bf16[80,640]{1,0:T(8,128)(2,1)} async-done(((bf16[1280,640]{1,0:T(8,128)(2,1)}), bf16[80,640]{1,0:T(8,128)(2,1)}) %reduce-scatter.63.cloned.1.call-update) | async-done | bytes 102416 | tf_op jit(solution)/shard_map/reduce_scatter | solution.py:258
  3391.6 78.3 %reduce-scatter.61.cloned.1.call-done = bf16[80,640]{1,0:T(8,128)(2,1)} async-done(((bf16[1280,640]{1,0:T(8,128)(2,1)}), bf16[80,640]{1,0:T(8,128)(2,1)}) %reduce-scatter.61.cloned.1.call-update) | async-done | bytes 102416 | tf_op jit(solution)/shard_map/reduce_scatter | solution.py:258
  3469.9 78.3 %reduce-scatter.59.cloned.1.call-done = bf16[80,640]{1,0:T(8,128)(2,1)} async-done(((bf16[1280,640]{1,0:T(8,128)(2,1)}), bf16[80,640]{1,0:T(8,128)(2,1)}) %reduce-scatter.59.cloned.1.call-update) | async-done | bytes 102416 | tf_op jit(solution)/shard_map/reduce_scatter | solution.py:258
  3548.2 78.4 %reduce-scatter.57.cloned.1.call-done = bf16[80,640]{1,0:T(8,128)(2,1)} async-done(((bf16[1280,640]{1,0:T(8,128)(2,1)}), bf16[80,640]{1,0:T(8,128)(2,1)}) %reduce-scatter.57.cloned.1.call-update) | async-done | bytes 102416 | tf_op jit(solution)/shard_map/reduce_scatter | solution.py:258
  3628.4 76.4 %reduce-scatter.71.cloned.1.call-done = bf16[80,640]{1,0:T(8,128)(2,1)} async-done(((bf16[1280,640]{1,0:T(8,128)(2,1)}), bf16[80,640]{1,0:T(8,128)(2,1)}) %reduce-scatter.71.cloned.1.call-update) | async-done | bytes 102416 | tf_op jit(solution)/shard_map/reduce_scatter | solution.py:261
  3704.8 78.4 %reduce-scatter.69.cloned.1.call-done = bf16[80,640]{1,0:T(8,128)(2,1)} async-done(((bf16[1280,640]{1,0:T(8,128)(2,1)}), bf16[80,640]{1,0:T(8,128)(2,1)}) %reduce-scatter.69.cloned.1.call-update) | async-done | bytes 102416 | tf_op jit(solution)/shard_map/reduce_scatter | solution.py:261
  3783.2 78.2 %reduce-scatter.67.cloned.1.call-done = bf16[80,640]{1,0:T(8,128)(2,1)} async-done(((bf16[1280,640]{1,0:T(8,128)(2,1)}), bf16[80,640]{1,0:T(8,128)(2,1)}) %reduce-scatter.67.cloned.1.call-update) | async-done | bytes 102416 | tf_op jit(solution)/shard_map/reduce_scatter | solution.py:261
  3861.4 78.4 %reduce-scatter.65.cloned.1.call-done = bf16[80,640]{1,0:T(8,128)(2,1)} async-done(((bf16[1280,640]{1,0:T(8,128)(2,1)}), bf16[80,640]{1,0:T(8,128)(2,1)}) %reduce-scatter.65.cloned.1.call-update) | async-done | bytes 102416 | tf_op jit(solution)/shard_map/reduce_scatter | solution.py:261
  (981 shorter events, 566.3 us)
Async XLA Ops:
  7.2 64.6 %all-gather.19.cloned.1.call-start = ((), (), s32[]{:S(2)}) async-start(), calls=%async_computation.32 | async-start | bytes 1740800 | tf_op jit(solution)/shard_map/all_gather | solution.py:58
  7.9 123.5 %all-gather.21.cloned.1.call-start = ((), (), s32[]{:S(2)}) async-start(), calls=%async_computation.33 | async-start | bytes 1740800 | tf_op jit(solution)/shard_map/all_gather | solution.py:59
  8.7 182.5 %all-gather.23.cloned.1.call-start = ((), (), s32[]{:S(2)}) async-start(), calls=%async_computation.34 | async-start | bytes 1740800 | tf_op jit(solution)/shard_map/all_gather | solution.py:60
  9.4 273.7 %all-gather.35.cloned.1.call-start = ((), (), s32[]{:S(2)}) async-start(), calls=%async_computation.40 | async-start | bytes 5570560 | tf_op jit(solution)/shard_map/all_gather | solution.py:86
  57.4 319.4 %copy-start.88 = (f32[1280]{0:T(1024)}, f32[1280]{0:T(1024)S(1)}, u32[]{:S(2)}) copy-start(f32[1280]{0:T(1024)S(1)} %convert_element_type.618) | copy-start | bytes 15364
  198.9 143.5 %all-gather.27.cloned.1.call-start = ((), (), s32[]{:S(2)}) async-start(), calls=%async_computation.36 | async-start | bytes 1740800 | tf_op jit(solution)/shard_map/all_gather | solution.py:64
  199.5 163.0 %all-reduce.21.cloned.1.call-start = ((), (), s32[]{:S(2)}) async-start(), calls=%async_computation.41 | async-start | bytes 655360 | tf_op jit(solution)/shard_map/psum | solution.py:118
  345.2 79.7 %all-gather.29.cloned.1.call-start = ((), (), s32[]{:S(2)}) async-start(), calls=%async_computation.37 | async-start | bytes 1740800 | tf_op jit(solution)/shard_map/all_gather | solution.py:61
  345.9 139.0 %all-gather.31.cloned.1.call-start = ((), (), s32[]{:S(2)}) async-start(), calls=%async_computation.38 | async-start | bytes 1740800 | tf_op jit(solution)/shard_map/all_gather | solution.py:65
  346.7 225.5 %all-gather.37.cloned.1.call-start = ((), (), s32[]{:S(2)}) async-start(), calls=%async_computation.42 | async-start | bytes 5570560 | tf_op jit(solution)/shard_map/all_gather | solution.py:86
  369.4 289.5 %all-gather.25.cloned.1.call-start = ((), (), s32[]{:S(2)}) async-start(), calls=%async_computation.35 | async-start | bytes 5570560 | tf_op jit(solution)/shard_map/all_gather | solution.py:86
  376.2 369.6 %all-gather.33.cloned.1.call-start = ((), (), s32[]{:S(2)}) async-start(), calls=%async_computation.39 | async-start | bytes 5570560 | tf_op jit(solution)/shard_map/all_gather | solution.py:86
  382.6 428.6 %all-reduce.27.cloned.1.call-start = ((), (), s32[]{:S(2)}) async-start(), calls=%async_computation.85 | async-start | bytes 2621440 | tf_op jit(solution)/shard_map/psum | solution.py:118
  385.3 661.5 %copy-start.149 = (f32[128]{0:T(128)}, f32[128]{0:T(128)S(1)}, u32[]{:S(2)}) copy-start(f32[128]{0:T(128)S(1)} %get-tuple-element.992) | copy-start | bytes 1540
  385.5 370.1 %copy-start.16 = (bf16[128,8,80]{0,2,1:T(8,128)(2,1)}, bf16[128,8,80]{0,2,1:T(8,128)(2,1)S(1)}, u32[]{:S(2)}) copy-start(bf16[128,8,80]{0,2,1:T(8,128)(2,1)S(1)} %get-tuple-element.1494) | copy-start | bytes 491524
  792.4 50.4 %all-reduce.25.cloned.1.call-start = ((), (), s32[]{:S(2)}) async-start(), calls=%async_computation.84 | async-start | bytes 1966080 | tf_op jit(solution)/shard_map/psum | solution.py:138
  821.8 89.7 %all-gather.51.cloned.1.call-start = ((), (), s32[]{:S(2)}) async-start(), calls=%async_computation.55 | async-start | bytes 2785280 | tf_op jit(solution)/shard_map/all_gather | solution.py:157
  823.7 154.4 %all-gather.53.cloned.1.call-start = ((), (), s32[]{:S(2)}) async-start(), calls=%async_computation.56 | async-start | bytes 2785280 | tf_op jit(solution)/shard_map/all_gather | solution.py:158
  824.3 229.7 %all-gather.39.cloned.1.call-start = ((), (), s32[]{:S(2)}) async-start(), calls=%async_computation.43 | async-start | bytes 2785280 | tf_op jit(solution)/shard_map/all_gather | solution.py:157
  826.1 284.9 %all-gather.41.cloned.1.call-start = ((), (), s32[]{:S(2)}) async-start(), calls=%async_computation.44 | async-start | bytes 2785280 | tf_op jit(solution)/shard_map/all_gather | solution.py:158
  826.7 363.3 %all-gather.43.cloned.1.call-start = ((), (), s32[]{:S(2)}) async-start(), calls=%async_computation.47 | async-start | bytes 2785280 | tf_op jit(solution)/shard_map/all_gather | solution.py:157
  828.5 414.4 %all-gather.45.cloned.1.call-start = ((), (), s32[]{:S(2)}) async-start(), calls=%async_computation.48 | async-start | bytes 2785280 | tf_op jit(solution)/shard_map/all_gather | solution.py:158
  829.3 492.0 %all-gather.47.cloned.1.call-start = ((), (), s32[]{:S(2)}) async-start(), calls=%async_computation.51 | async-start | bytes 2785280 | tf_op jit(solution)/shard_map/all_gather | solution.py:157
  831.1 543.8 %all-gather.49.cloned.1.call-start = ((), (), s32[]{:S(2)}) async-start(), calls=%async_computation.52 | async-start | bytes 2785280 | tf_op jit(solution)/shard_map/all_gather | solution.py:158
  832.3 663.8 %reduce-scatter.47.cloned.1.call-start = ((), (), s32[]{:S(2)}) async-start(), calls=%async_computation.58 | async-start | bytes 2785280 | tf_op jit(solution)/shard_map/reduce_scatter | solution.py:215
  1046.8 493.9 %reduce-scatter.45.cloned.1.call-start = ((), (), s32[]{:S(2)}) async-start(), calls=%async_computation.57 | async-start | bytes 2785280 | tf_op jit(solution)/shard_map/reduce_scatter | solution.py:209
  1052.9 569.7 %reduce-scatter.35.cloned.1.call-start = ((), (), s32[]{:S(2)}) async-start(), calls=%async_computation.46 | async-start | bytes 2785280 | tf_op jit(solution)/shard_map/reduce_scatter | solution.py:215
  1186.1 518.6 %reduce-scatter.33.cloned.1.call-start = ((), (), s32[]{:S(2)}) async-start(), calls=%async_computation.45 | async-start | bytes 2785280 | tf_op jit(solution)/shard_map/reduce_scatter | solution.py:209
  1189.0 597.4 %reduce-scatter.39.cloned.1.call-start = ((), (), s32[]{:S(2)}) async-start(), calls=%async_computation.50 | async-start | bytes 2785280 | tf_op jit(solution)/shard_map/reduce_scatter | solution.py:215
  1317.4 550.5 %reduce-scatter.37.cloned.1.call-start = ((), (), s32[]{:S(2)}) async-start(), calls=%async_computation.49 | async-start | bytes 2785280 | tf_op jit(solution)/shard_map/reduce_scatter | solution.py:209
  1320.2 629.6 %reduce-scatter.43.cloned.1.call-start = ((), (), s32[]{:S(2)}) async-start(), calls=%async_computation.54 | async-start | bytes 2785280 | tf_op jit(solution)/shard_map/reduce_scatter | solution.py:215
  1449.9 582.0 %reduce-scatter.41.cloned.1.call-start = ((), (), s32[]{:S(2)}) async-start(), calls=%async_computation.53 | async-start | bytes 2785280 | tf_op jit(solution)/shard_map/reduce_scatter | solution.py:209
  1450.6 659.8 %reduce-scatter.85.cloned.1.call-start = ((), (), s32[]{:S(2)}) async-start(), calls=%async_computation.77 | async-start | bytes 1740800 | tf_op jit(solution)/shard_map/reduce_scatter | solution.py:264
  1453.1 735.7 %reduce-scatter.87.cloned.1.call-start = ((), (), s32[]{:S(2)}) async-start(), calls=%async_computation.78 | async-start | bytes 1740800 | tf_op jit(solution)/shard_map/reduce_scatter | solution.py:264
  1455.2 812.0 %reduce-scatter.83.cloned.1.call-start = ((), (), s32[]{:S(2)}) async-start(), calls=%async_computation.76 | async-start | bytes 1740800 | tf_op jit(solution)/shard_map/reduce_scatter | solution.py:264
  1457.2 888.3 %reduce-scatter.81.cloned.1.call-start = ((), (), s32[]{:S(2)}) async-start(), calls=%async_computation.75 | async-start | bytes 1740800 | tf_op jit(solution)/shard_map/reduce_scatter | solution.py:264
  1459.3 964.5 %reduce-scatter.93.cloned.1.call-start = ((), (), s32[]{:S(2)}) async-start(), calls=%async_computation.81 | async-start | bytes 1740800 | tf_op jit(solution)/shard_map/reduce_scatter | solution.py:276
  1462.3 1040.1 %reduce-scatter.95.cloned.1.call-start = ((), (), s32[]{:S(2)}) async-start(), calls=%async_computation.82 | async-start | bytes 1740800 | tf_op jit(solution)/shard_map/reduce_scatter | solution.py:276
  1465.2 1115.4 %reduce-scatter.91.cloned.1.call-start = ((), (), s32[]{:S(2)}) async-start(), calls=%async_computation.80 | async-start | bytes 1740800 | tf_op jit(solution)/shard_map/reduce_scatter | solution.py:276
  1468.0 1191.0 %reduce-scatter.89.cloned.1.call-start = ((), (), s32[]{:S(2)}) async-start(), calls=%async_computation.79 | async-start | bytes 1740800 | tf_op jit(solution)/shard_map/reduce_scatter | solution.py:276
  1471.0 1266.4 %reduce-scatter.79.cloned.1.call-start = ((), (), s32[]{:S(2)}) async-start(), calls=%async_computation.74 | async-start | bytes 1740800 | tf_op jit(solution)/shard_map/reduce_scatter | solution.py:273
  1473.8 1341.9 %reduce-scatter.77.cloned.1.call-start = ((), (), s32[]{:S(2)}) async-start(), calls=%async_computation.73 | async-start | bytes 1740800 | tf_op jit(solution)/shard_map/reduce_scatter | solution.py:273
  1476.8 1417.3 %reduce-scatter.75.cloned.1.call-start = ((), (), s32[]{:S(2)}) async-start(), calls=%async_computation.72 | async-start | bytes 1740800 | tf_op jit(solution)/shard_map/reduce_scatter | solution.py:273
  1479.7 1492.9 %reduce-scatter.73.cloned.1.call-start = ((), (), s32[]{:S(2)}) async-start(), calls=%async_computation.71 | async-start | bytes 1740800 | tf_op jit(solution)/shard_map/reduce_scatter | solution.py:273
  1484.4 1511.0 %all-reduce.23.cloned.1.call-start = ((), (), s32[]{:S(2)}) async-start(), calls=%async_computation.83 | async-start | bytes 5242880 | tf_op jit(solution)/shard_map/psum | solution.py:127
  2036.7 1045.9 %reduce-scatter.55.cloned.1.call-start = ((), (), s32[]{:S(2)}) async-start(), calls=%async_computation.62 | async-start | bytes 1740800 | tf_op jit(solution)/shard_map/reduce_scatter | solution.py:255
  2041.9 1114.8 %reduce-scatter.53.cloned.1.call-start = ((), (), s32[]{:S(2)}) async-start(), calls=%async_computation.61 | async-start | bytes 1740800 | tf_op jit(solution)/shard_map/reduce_scatter | solution.py:255
  2046.0 1188.9 %reduce-scatter.51.cloned.1.call-start = ((), (), s32[]{:S(2)}) async-start(), calls=%async_computation.60 | async-start | bytes 1740800 | tf_op jit(solution)/shard_map/reduce_scatter | solution.py:255
  2050.1 1263.4 %reduce-scatter.49.cloned.1.call-start = ((), (), s32[]{:S(2)}) async-start(), calls=%async_computation.59 | async-start | bytes 1740800 | tf_op jit(solution)/shard_map/reduce_scatter | solution.py:255
  2054.3 1337.3 %reduce-scatter.63.cloned.1.call-start = ((), (), s32[]{:S(2)}) async-start(), calls=%async_computation.66 | async-start | bytes 1740800 | tf_op jit(solution)/shard_map/reduce_scatter | solution.py:258
  2054.9 1415.0 %reduce-scatter.61.cloned.1.call-start = ((), (), s32[]{:S(2)}) async-start(), calls=%async_computation.65 | async-start | bytes 1740800 | tf_op jit(solution)/shard_map/reduce_scatter | solution.py:258
  2055.5 1492.7 %reduce-scatter.59.cloned.1.call-start = ((), (), s32[]{:S(2)}) async-start(), calls=%async_computation.64 | async-start | bytes 1740800 | tf_op jit(solution)/shard_map/reduce_scatter | solution.py:258
  2056.1 1570.6 %reduce-scatter.57.cloned.1.call-start = ((), (), s32[]{:S(2)}) async-start(), calls=%async_computation.63 | async-start | bytes 1740800 | tf_op jit(solution)/shard_map/reduce_scatter | solution.py:258
  2056.8 1648.0 %reduce-scatter.71.cloned.1.call-start = ((), (), s32[]{:S(2)}) async-start(), calls=%async_computation.70 | async-start | bytes 1740800 | tf_op jit(solution)/shard_map/reduce_scatter | solution.py:261
  2057.4 1725.8 %reduce-scatter.69.cloned.1.call-start = ((), (), s32[]{:S(2)}) async-start(), calls=%async_computation.69 | async-start | bytes 1740800 | tf_op jit(solution)/shard_map/reduce_scatter | solution.py:261
  2058.1 1803.2 %reduce-scatter.67.cloned.1.call-start = ((), (), s32[]{:S(2)}) async-start(), calls=%async_computation.68 | async-start | bytes 1740800 | tf_op jit(solution)/shard_map/reduce_scatter | solution.py:261
  2058.7 1881.1 %reduce-scatter.65.cloned.1.call-start = ((), (), s32[]{:S(2)}) async-start(), calls=%async_computation.67 | async-start | bytes 1740800 | tf_op jit(solution)/shard_map/reduce_scatter | solution.py:261
  2347.3 650.1 %copy-start.131 = (bf16[1280]{0:T(1024)(128)(2,1)S(1)}, bf16[1280]{0:T(1024)(128)(2,1)}, u32[]{:S(2)}) copy-start(bf16[1280]{0:T(1024)(128)(2,1)} %get-tuple-element.739) | copy-start | bytes 7684
  2347.3 650.1 %copy-start.132 = (bf16[1280]{0:T(1024)(128)(2,1)S(1)}, bf16[1280]{0:T(1024)(128)(2,1)}, u32[]{:S(2)}) copy-start(bf16[1280]{0:T(1024)(128)(2,1)} %get-tuple-element.741) | copy-start | bytes 7684
  2347.3 650.2 %copy-start.133 = (bf16[1280]{0:T(1024)(128)(2,1)S(1)}, bf16[1280]{0:T(1024)(128)(2,1)}, u32[]{:S(2)}) copy-start(bf16[1280]{0:T(1024)(128)(2,1)} %get-tuple-element.758) | copy-start | bytes 7684
  2347.3 650.2 %copy-start.134 = (bf16[1280]{0:T(1024)(128)(2,1)S(1)}, bf16[1280]{0:T(1024)(128)(2,1)}, u32[]{:S(2)}) copy-start(bf16[1280]{0:T(1024)(128)(2,1)} %get-tuple-element.760) | copy-start | bytes 7684
  2660.8 415.1 %copy-start.42 = (bf16[128,1280]{1,0:T(8,128)(2,1)S(1)}, bf16[128,1280]{1,0:T(8,128)(2,1)}, u32[]{:S(2)}) copy-start(bf16[128,1280]{1,0:T(8,128)(2,1)} %all-reduce.21.cloned.1.call-done) | copy-start | bytes 983044
  2660.8 415.2 %copy-start.46 = (f32[128,1280]{1,0:T(8,128)S(1)}, f32[128,1280]{1,0:T(8,128)}, u32[]{:S(2)}) copy-start(f32[128,1280]{1,0:T(8,128)} %copy-done.44) | copy-start | bytes 1966084
  2660.8 415.2 %copy-start.151 = (f32[128]{0:T(128)S(1)}, f32[128]{0:T(128)}, u32[]{:S(2)}) copy-start(f32[128]{0:T(128)} %get-tuple-element.989) | copy-start | bytes 1540
  (196 other events, 1813.8 us)
Sparse Core Ops, SparseCore 0:
  10.7 61.0 all-gather.18
  74.4 56.9 all-gather.20
  134.1 56.9 all-gather.22
  199.0 84.0 all-gather.34
  285.7 56.6 all-gather.26
  345.3 17.2 all-reduce.20
  365.6 59.2 all-gather.28
  427.9 56.9 all-gather.30
  488.1 84.0 all-gather.36
  575.1 83.7 all-gather.24
  662.0 83.7 all-gather.32
  792.5 18.6 all-reduce.26
  822.0 20.8 all-reduce.24
  846.3 65.2 all-gather.50
  915.0 62.9 all-gather.52
  981.5 63.0 all-gather.38
  1048.0 62.9 all-gather.40
  1113.9 62.9 all-gather.42
  1180.0 62.9 all-gather.44
  1245.8 62.9 all-gather.46
  1311.9 62.9 all-gather.48
  1377.3 80.8 reduce-scatter.46
  1461.2 79.4 reduce-scatter.44
  1542.9 79.6 reduce-scatter.34
  1625.1 79.6 reduce-scatter.32
  1707.0 79.3 reduce-scatter.38
  1788.6 79.2 reduce-scatter.36
  1870.2 79.5 reduce-scatter.42
  1952.2 79.5 reduce-scatter.40
  2034.1 76.3 reduce-scatter.84
  2112.7 76.0 reduce-scatter.86
  2191.2 75.9 reduce-scatter.82
  2269.4 76.0 reduce-scatter.80
  2347.9 75.9 reduce-scatter.92
  2426.2 76.0 reduce-scatter.94
  2504.5 76.0 reduce-scatter.90
  2582.7 76.2 reduce-scatter.88
  2661.4 75.9 reduce-scatter.78
  2739.5 76.0 reduce-scatter.76
  2818.0 76.0 reduce-scatter.74
  2896.4 76.0 reduce-scatter.72
  2976.2 19.0 all-reduce.22
  2997.5 80.7 reduce-scatter.54
  3080.6 76.0 reduce-scatter.52
  3158.8 76.0 reduce-scatter.50
  3237.1 76.2 reduce-scatter.48
  3315.6 75.9 reduce-scatter.62
  3393.8 76.0 reduce-scatter.60
  3472.1 76.1 reduce-scatter.58
  3550.6 75.9 reduce-scatter.56
  3628.8 75.9 reduce-scatter.70
  3707.2 75.9 reduce-scatter.68
  3785.3 76.0 reduce-scatter.66
  3863.8 75.9 reduce-scatter.64
